TPU v7x, 128 devices: a whole 4x4x4 slice. The times are simulated.
128 devices in a mesh: sx: 8 (over z, core), sy: 16 (over x, y).
Axes of the slice: x: 4, y: 4, z: 4, core: 2. Of those that a mesh axis runs over, the one named last changes fastest.
Arguments:
- fine_matrix: bfloat16 [16, 32, 2, 7, 64, 64], P('sx', 'sy'), may hold values from -0.75 to 0.75
- prolongator: bfloat16 [16, 32, 2, 7, 64, 64], P('sx', 'sy'), may hold values from -2.5 to 2.5
- aggregate: int32 [16, 32, 2], P('sx', 'sy'), may hold values from 0 to 127, as said below
- face_links: int32 [16, 32, 2, 6], P('sx', 'sy'), may hold values from 0 to 1, as said below
Outputs:
- coarse: bfloat16 [8, 16, 7, 7, 64, 64], P('sx', 'sy')
Inputs may be any that keep to these rules, and one draw needn't show every extreme that they name: aggregate[i] is the id bx 16 + by of a box of 2 x 2 x 2 elements: the box that holds element i, or the box beside it across a box face on which element i lies (faces along x or y). face_links[i, f] is the same on both sides of a face, and 0 on the outer faces of the grid.
All inputs are finite; a program needn't handle non-finite values.
Results may differ from a plain program's by a relative error of at most 0.007.
Values may be sent and summed in bfloat16 or wider, within the bound.
A program may use at most 320 MiB of HBM per device.

v0:
```python
import jax
import jax.numpy as jnp
from jax import lax
from jax.sharding import PartitionSpec as P


def extended_2(cells, sides, width):
    for axis, dim in sides:
        count = lax.axis_size(axis)
        ends = count - 1
        head = lax.slice_in_dim(cells, 0, width, axis=dim)
        tail = lax.slice_in_dim(cells, cells.shape[dim] - width, cells.shape[dim], axis=dim)
        cells = jnp.concatenate(
            [
                lax.ppermute(tail, axis, [(i, (i + 1) % count) for i in range(ends)]),
                cells,
                lax.ppermute(head, axis, [((i + 1) % count, i) for i in range(ends)]),
            ],
            axis=dim,
        )
    return cells


def from_behind(value, axis, by):
    size = lax.axis_size(axis)
    pairs = [(i, i + by) for i in range(size) if 0 <= i + by < size]
    return lax.ppermute(value, axis, pairs)


def neighbour_views(extended):
    padded = jnp.pad(extended, [(0, 0), (0, 0), (1, 1)] + [(0, 0)] * (extended.ndim - 3))
    return [
        padded[1:-1, 1:-1, 1:3],
        padded[:-2, 1:-1, 1:3],
        padded[2:, 1:-1, 1:3],
        padded[1:-1, :-2, 1:3],
        padded[1:-1, 2:, 1:3],
        padded[1:-1, 1:-1, 0:2],
        padded[1:-1, 1:-1, 2:4],
    ]


def slot_ids(aggregate_ext, face_links, first_x, first_y, boxes_y):
    neighbours = jnp.stack(neighbour_views(aggregate_ext), axis=-1)
    count_x, count_y = (face_links.shape[0], face_links.shape[1])
    box_x = ((first_x + jnp.arange(count_x, dtype=jnp.int32)) // 2)[:, None, None, None]
    box_y = ((first_y + jnp.arange(count_y, dtype=jnp.int32)) // 2)[None, :, None, None]
    target_x = neighbours // boxes_y
    target_y = neighbours % boxes_y
    within = (target_x - box_x + 1) * 3 + (target_y - box_y + 1)
    present = jnp.concatenate([jnp.ones_like(face_links[..., :1]), face_links], axis=-1) == 1
    return jnp.where(present, within, -1)


def combine_rows(slot_table, blocks):
    selector = (slot_table[..., None] == jnp.arange(9, dtype=jnp.int32)).astype(blocks.dtype)
    combined = jnp.einsum(
        "xyzmt,xyzmpq->xyztpq", selector, blocks, preferred_element_type=jnp.float32
    )
    return combined.astype(jnp.bfloat16)


def box_step(direction, parity_x, parity_y):
    shift_x = 0
    shift_y = 0
    if direction == 1 and parity_x == 0:
        shift_x = -1
    if direction == 2 and parity_x == 1:
        shift_x = 1
    if direction == 3 and parity_y == 0:
        shift_y = -1
    if direction == 4 and parity_y == 1:
        shift_y = 1
    return (shift_x, shift_y)


def image_blocks(fine_matrix, face_links, box_ext):
    views = neighbour_views(box_ext)
    count_x, count_y = (fine_matrix.shape[0], fine_matrix.shape[1])
    half_x, half_y = (count_x // 2, count_y // 2)
    width, coarse_width = (fine_matrix.shape[-1], box_ext.shape[-1])
    total = jnp.zeros((half_x, 2, half_y, 2, 2, 5, 5, width, coarse_width), jnp.float32)
    for direction in range(7):
        product = jnp.einsum(
            "xyzpq,xyztqr->xyztpr",
            fine_matrix[:, :, :, direction],
            views[direction],
            preferred_element_type=jnp.float32,
        )
        if direction > 0:
            product = product * face_links[:, :, :, direction - 1, None, None, None].astype(
                jnp.float32
            )
        product = product.reshape(half_x, 2, half_y, 2, 2, 3, 3, width, coarse_width)
        for parity_x in range(2):
            for parity_y in range(2):
                shift_x, shift_y = box_step(direction, parity_x, parity_y)
                total = total.at[
                    :,
                    parity_x,
                    :,
                    parity_y,
                    :,
                    1 + shift_x : 4 + shift_x,
                    1 + shift_y : 4 + shift_y,
                ].add(product[:, parity_x, :, parity_y])
    return total.astype(jnp.bfloat16).reshape(half_x, 2, half_y, 2, 2, 25, width, coarse_width)


def place_blocks(contrib):
    half_x, half_y = (contrib.shape[0], contrib.shape[1])
    coarse_width = contrib.shape[-1]
    buffer = jnp.zeros((half_x + 2, half_y + 2, 7, 7, coarse_width, coarse_width), jnp.float32)
    for offset_x in range(3):
        for offset_y in range(3):
            piece = contrib[:, :, 3 * offset_x + offset_y].reshape(
                half_x, half_y, 5, 5, coarse_width, coarse_width
            )
            buffer = buffer.at[
                offset_x : offset_x + half_x,
                offset_y : offset_y + half_y,
                2 - offset_x : 7 - offset_x,
                2 - offset_y : 7 - offset_y,
            ].add(piece)
    return buffer


def per_device(fine_matrix, prolongator, aggregate, face_links):
    count_x, count_y = (aggregate.shape[0], aggregate.shape[1])
    half_x, half_y = (count_x // 2, count_y // 2)
    width, coarse_width = (fine_matrix.shape[-1], prolongator.shape[-1])
    first_x = lax.axis_index("sx") * count_x
    first_y = lax.axis_index("sy") * count_y
    boxes_y = count_y * lax.axis_size("sy") // 2
    aggregate_ext = extended_2(aggregate, (("sx", 0), ("sy", 1)), 1)
    slot_table = slot_ids(aggregate_ext, face_links, first_x, first_y, boxes_y)
    ghost_blocks = extended_2(prolongator, (("sx", 0), ("sy", 1)), 1)
    ghost_table = extended_2(slot_table, (("sx", 0), ("sy", 1)), 1)
    box_ext = combine_rows(ghost_table, ghost_blocks)
    box_own = box_ext[1:-1, 1:-1]
    image = image_blocks(fine_matrix, face_links, box_ext)
    left = box_own.reshape(half_x, 2, half_y, 2, 2, 9, width, coarse_width)
    contrib = jnp.einsum(
        "abcderkp,abcdeskq->acrspq", left, image, preferred_element_type=jnp.float32
    )
    buffer = place_blocks(contrib)
    lower_y = buffer[:, 0]
    upper_y = buffer[:, half_y + 1]
    from_right = from_behind(lower_y, "sy", -1)
    from_left = from_behind(upper_y, "sy", 1)
    inner = buffer[:, 1 : half_y + 1]
    inner = inner.at[:, half_y - 1].add(from_right)
    inner = inner.at[:, 0].add(from_left)
    lower_x = inner[0]
    upper_x = inner[half_x + 1]
    from_above = from_behind(lower_x.astype(jnp.bfloat16), "sx", -1).astype(lower_x.dtype)
    from_below = from_behind(upper_x.astype(jnp.bfloat16), "sx", 1).astype(upper_x.dtype)
    owned = inner[1 : half_x + 1]
    owned = owned.at[half_x - 1].add(from_above)
    owned = owned.at[0].add(from_below)
    return owned.astype(jnp.bfloat16)


def solution(mesh):
    return jax.shard_map(
        per_device,
        mesh=mesh,
        in_specs=(
            P("sx", "sy", None, None, None, None),
            P("sx", "sy", None, None, None, None),
            P("sx", "sy", None),
            P("sx", "sy", None, None),
        ),
        out_specs=P("sx", "sy", None, None, None, None),
        check_vma=False,
    )
```

profile of v0, /device:TPU:39, one launch (start us, length us, event | category | flops | bytes accessed | tf_op | source)
XLA Modules:
  0.0 257.3 jit_solution(12386212315452902597)
XLA Ops:
  0.0 0.9 copy.123
  0.9 2.6 %collective-permute-start.1 = (s32[1,2,2]{0,2,1:T(2,128)S(1)}, s32[1,2,2]{0,2,1:T(2,128)S(1)}, u32[]{:S(2)}, u32[]{:S(2)}) collective-permute-start(s32[1,2,2]{0,2,1:T(2,128)S(1)} %get-tuple-element.542), channel_id=1, source_target_pairs={{16,0},{32,16},{48,32},{64,48},{80,64},{96,80},{112,96},{17,1},{33... | collective-permute-start | bytes 56 | tf_op jit(solution)/shard_map/ppermute | solution.py:17
  3.5 3.4 %collective-permute-start = (s32[1,2,2]{0,2,1:T(2,128)S(1)}, s32[1,2,2]{0,2,1:T(2,128)S(1)}, u32[]{:S(2)}, u32[]{:S(2)}) collective-permute-start(s32[1,2,2]{0,2,1:T(2,128)S(1)} %get-tuple-element.543), channel_id=1, source_target_pairs={{0,16},{16,32},{32,48},{48,64},{64,80},{80,96},{96,112},{1,17},{17... | collective-permute-start | bytes 56 | tf_op jit(solution)/shard_map/ppermute | solution.py:15
  7.0 1.2 fusion.81
  8.5 2.4 collective-permute-start.8
  11.2 1.9 collective-permute-start.9
  13.2 0.8 copy.132
  14.3 0.7 fusion.74
  15.2 4.9 %collective-permute-start.3 = (s32[4,1,2]{0,2,1:T(2,128)S(1)}, s32[4,1,2]{0,2,1:T(2,128)S(1)}, u32[]{:S(2)}, u32[]{:S(2)}) collective-permute-start(s32[4,1,2]{0,2,1:T(2,128)S(1)} %get-tuple-element.538), channel_id=1, source_target_pairs={{1,0},{2,1},{3,2},{4,3},{5,4},{6,5},{7,6},{8,7},{9,8},{10,9},{11,1... | collective-permute-start | bytes 104 | tf_op jit(solution)/shard_map/ppermute | solution.py:17
  20.1 1.9 collective-permute-start.2
  22.0 4.5 %collective-permute-done.2 = s32[4,1,2]{0,2,1:T(2,128)S(1)} collective-permute-done((s32[4,1,2]{0,2,1:T(2,128)S(1)}, s32[4,1,2]{0,2,1:T(2,128)S(1)}, u32[]{:S(2)}, u32[]{:S(2)}) %collective-permute-start.2) | collective-permute-done | bytes 64 | tf_op jit(solution)/shard_map/ppermute | solution.py:15
  27.3 0.8 compare_select_fusion
  28.1 5.1 %collective-permute-start.4 = (s32[1,2,2,7]{3,2,1,0:T(2,128)S(1)}, s32[1,2,2,7]{3,2,1,0:T(2,128)S(1)}, u32[]{:S(2)}, u32[]{:S(2)}) collective-permute-start(s32[1,2,2,7]{3,2,1,0:T(2,128)S(1)} %get-tuple-element.534), channel_id=1, source_target_pairs={{0,16},{16,32},{32,48},{48,64},{64,80},{80,96},{96,112},{1,17},{17... | collective-permute-start | bytes 344 | tf_op jit(solution)/shard_map/ppermute | solution.py:15
  33.2 1.9 collective-permute-start.5
  36.6 1.9 collective-permute-start.11
  38.5 3.4 %collective-permute-start.10 = (bf16[4,1,2,7,64,64]{5,4,3,2,1,0:T(8,128)(2,1)S(1)}, bf16[4,1,2,7,64,64]{5,4,3,2,1,0:T(8,128)(2,1)S(1)}, u32[]{:S(2)}, u32[]{:S(2)}) collective-permute-start(bf16[4,1,2,7,64,64]{5,4,3,2,1,0:T(8,128)(2,1)S(1)} %copy.142), channel_id=1, source_target_pairs={{0,1},{1,2},{2,3},{3,4},{4,5},{5,6},{6,7},{7,8},{8,9},{9,10},{10,1... | collective-permute-start | bytes 1376264 | tf_op jit(solution)/shard_map/ppermute | solution.py:15
  42.0 1.9 collective-permute-start.6
  43.9 5.5 %collective-permute-start.7 = (s32[4,1,2,7]{3,2,1,0:T(2,128)S(1)}, s32[4,1,2,7]{3,2,1,0:T(2,128)S(1)}, u32[]{:S(2)}, u32[]{:S(2)}) collective-permute-start(s32[4,1,2,7]{3,2,1,0:T(2,128)S(1)} %get-tuple-element.531), channel_id=1, source_target_pairs={{1,0},{2,1},{3,2},{4,3},{5,4},{6,5},{7,6},{8,7},{9,8},{10,9},{11,1... | collective-permute-start | bytes 680 | tf_op jit(solution)/shard_map/ppermute | solution.py:17
  49.6 14.8 %collective-permute-done.6 = s32[4,1,2,7]{3,2,1,0:T(2,128)S(1)} collective-permute-done((s32[4,1,2,7]{3,2,1,0:T(2,128)S(1)}, s32[4,1,2,7]{3,2,1,0:T(2,128)S(1)}, u32[]{:S(2)}, u32[]{:S(2)}) %collective-permute-start.6) | collective-permute-done | bytes 256 | tf_op jit(solution)/shard_map/ppermute | solution.py:15
  65.7 5.6 %convolution_convert_fusion = bf16[4,4,2,9,64,64]{5,3,4,2,1,0:T(8,128)(2,1)S(1)} fusion(bf16[4,1,2,7,64,64]{5,3,4,2,1,0:T(8,128)(2,1)S(1)} %copy.145, bf16[4,2,2,7,64,64]{5,3,4,2,1,0:T(8,128)(2,1)S(1)} %constant_dynamic-update-slice_fusion.1, bf16[4,1,2,7,64,64]{5,3,4,2,1,0:T(8,128)(2,1)S(1)} %copy.144, s32[4,4,2,7]{3,2,1,0:T(2,128)S(1)} %pad_add_fusion), kind=kOutput, calls=%fused_computation.3 | convolution fusion | flops 23201760 | bytes 4195200 | tf_op jit(solution)/shard_map/xyzmt,xyzmpq->xyztpq/dot_general | solution.py:57
  71.2 5.7 %slice_bitcast_fusion.4 = (bf16[2,2,2,9,64,64,1]{5,3,4,2,1,0,6:T(8,128)(2,1)}, bf16[2,2,2,9,64,64]{5,3,4,2,1,0:T(8,128)(2,1)S(1)}, bf16[2,2,2,9,64,64]{5,3,4,2,1...) fusion(bf16[4,4,2,9,64,64]{5,3,4,2,1,0:T(8,128)(2,1)S(1)} %conv, ...), kind=kLoop, calls=%fused_computation.165 | loop fusion | bytes 23592960 | tf_op jit(solution)/shard_map/slice | solution.py:33
  76.9 1.4 fusion.17
  78.4 0.8 scatter-add.124
  87.1 0.8 convert_element_type.117
  88.0 0.7 copy.160
  88.7 0.8 copy-done.8
  89.6 2.8 %fusion.9 = f32[25,64,9,64,1,1,1]{3,1,6,5,0,2,4:T(8,128)S(1)} fusion(bf16[2,2,2,25,64,64,1]{4,5,2,1,3,6,0:T(8,128)(2,1)S(1)} %bitcast.182, bf16[2,2,2,9,64,64,1]{5,3,4,2,1,0,6:T(8,128)(2,1)S(1)} %copy-done.8), kind=kOutput, calls=%fused_computation.23 | convolution fusion | flops 943718400 | bytes 5914624 | tf_op jit(solution)/shard_map/abcderkp,abcdeskq->acrspq/dot_general | solution.py:143
  92.4 1.4 copy.220
  93.8 2.4 fusion.79
  96.2 2.3 copy.170
  98.5 2.4 copy.169
  100.9 2.3 copy.168
  103.2 2.3 copy.167
  105.5 2.3 copy.166
  107.9 1.2 copy.165
  109.9 1.8 scatter-add.170
  114.5 5.3 %slice_bitcast_fusion.1 = (f32[3,7,7,64,64]{4,3,2,1,0:T(8,128)}, f32[3,7,7,64,64]{4,3,2,1,0:T(8,128)}) fusion(f32[3,3,7,7,64,64]{5,4,3,2,0,1:T(8,128)S(1)} %fusion.19), kind=kLoop, calls=%fused_computation.5 | loop fusion | bytes 9633792 | tf_op jit(solution)/shard_map/squeeze | solution.py:147
  119.8 3.5 %copy-done = f32[3,3,7,7,64,64]{5,4,3,2,0,1:T(8,128)} copy-done((f32[3,3,7,7,64,64]{5,4,3,2,0,1:T(8,128)}, f32[3,3,7,7,64,64]{5,4,3,2,0,1:T(8,128)S(1)}, u32[]{:S(2)}) %copy-start) | copy-done | bytes 7225368
  123.3 1.9 collective-permute-start.12
  125.2 3.4 %collective-permute-start.13 = (f32[3,7,7,64,64]{4,3,2,1,0:T(8,128)}, f32[3,7,7,64,64]{4,3,2,1,0:T(8,128)}, u32[]{:S(2)}, u32[]{:S(2)}) collective-permute-start(f32[3,7,7,64,64]{4,3,2,1,0:T(8,128)} %get-tuple-element.506), channel_id=1, source_target_pairs={{0,1},{1,2},{2,3},{3,4},{4,5},{5,6},{6,7},{7,8},{8,9},{9,10},{10,1... | collective-permute-start | bytes 7225352 | tf_op jit(solution)/shard_map/ppermute | solution.py:27
  128.6 101.3 %collective-permute-done.12 = f32[3,7,7,64,64]{4,3,2,1,0:T(8,128)S(1)} collective-permute-done((f32[3,7,7,64,64]{4,3,2,1,0:T(8,128)}, f32[3,7,7,64,64]{4,3,2,1,0:T(8,128)S(1)}, u32[]{:S(2)}, u32[]{:S(2)}) %collective-permute-start.12) | collective-permute-done | bytes 2408480 | tf_op jit(solution)/shard_map/ppermute | solution.py:27
  229.9 4.0 %collective-permute-done.13 = f32[3,7,7,64,64]{4,3,2,1,0:T(8,128)} collective-permute-done((f32[3,7,7,64,64]{4,3,2,1,0:T(8,128)}, f32[3,7,7,64,64]{4,3,2,1,0:T(8,128)}, u32[]{:S(2)}, u32[]{:S(2)}) %collective-permute-start.13) | collective-permute-done | bytes 2408480 | tf_op jit(solution)/shard_map/ppermute | solution.py:27
  233.9 6.2 %fusion.77 = (bf16[3,1,7,7,64,64]{5,4,3,2,1,0:T(8,128)(2,1)S(1)}, f32[3,1,7,7,64,64]{5,4,3,2,1,0:T(8,128)S(1)}) fusion(f32[3,7,7,64,64]{4,3,2,1,0:T(8,128)} %collective-permute-done.13, f32[3,7,7,64,64]{4,3,2,1,0:T(8,128)S(1)} %collective-permute-done.12, f32[3,3,7,7,64,64]{5,4,3,2,0,1:T(8,128)} %copy-done), kind=kLoop, calls=%fused_computation.166 | loop fusion | flops 1806336 | bytes 10838016 | tf_op jit(solution)/shard_map/convert.3
  240.2 3.9 %collective-permute-start.14 = (bf16[1,7,7,64,64]{4,3,2,1,0:T(8,128)(2,1)S(1)}, bf16[1,7,7,64,64]{4,3,2,1,0:T(8,128)(2,1)S(1)}, u32[]{:S(2)}, u32[]{:S(2)}) collective-permute-start(bf16[1,7,7,64,64]{4,3,2,1,0:T(8,128)(2,1)S(1)} %get-tuple-element.524), channel_id=1, source_target_pairs={{16,0},{32,16},{48,32},{64,48},{80,64},{96,80},{112,96},{17,1},{33... | collective-permute-start | bytes 1204232 | tf_op jit(solution)/shard_map/ppermute | solution.py:27
  244.1 2.8 %collective-permute-start.15 = (bf16[1,7,7,64,64]{4,3,2,1,0:T(8,128)(2,1)S(1)}, bf16[1,7,7,64,64]{4,3,2,1,0:T(8,128)(2,1)S(1)}, u32[]{:S(2)}, u32[]{:S(2)}) collective-permute-start(bf16[1,7,7,64,64]{4,3,2,1,0:T(8,128)(2,1)S(1)} %get-tuple-element.525), channel_id=1, source_target_pairs={{0,16},{16,32},{32,48},{48,64},{64,80},{80,96},{96,112},{1,17},{17... | collective-permute-start | bytes 1204232 | tf_op jit(solution)/shard_map/ppermute | solution.py:27
  246.9 8.2 %collective-permute-done.14 = bf16[1,7,7,64,64]{4,3,2,1,0:T(8,128)(2,1)S(1)} collective-permute-done((bf16[1,7,7,64,64]{4,3,2,1,0:T(8,128)(2,1)S(1)}, bf16[1,7,7,64,64]{4,3,2,1,0:T(8,128)(2,1)S(1)}, u32[]{:S(2)}, u32[]{:S(2)}) %collective-permute-start.14) | collective-permute-done | bytes 401440 | tf_op jit(solution)/shard_map/ppermute | solution.py:27
  255.1 0.9 collective-permute-done.15
  256.0 1.3 fusion.8
  (107 shorter events, 16.3 us)
Async XLA Ops:
  0.0 35.2 %copy-start.1 = (bf16[2,2,2,7,64,64]{5,4,3,2,1,0:T(8,128)(2,1)S(1)}, bf16[2,2,2,7,64,64]{5,4,3,2,1,0:T(8,128)(2,1)}, u32[]{:S(2)}) copy-start(bf16[2,2,2,7,64,64]{5,4,3,2,1,0:T(8,128)(2,1)} %param.87) | copy-start | bytes 1376260
  0.9 13.0 %collective-permute-start.1 = (s32[1,2,2]{0,2,1:T(2,128)S(1)}, s32[1,2,2]{0,2,1:T(2,128)S(1)}, u32[]{:S(2)}, u32[]{:S(2)}) collective-permute-start(s32[1,2,2]{0,2,1:T(2,128)S(1)} %get-tuple-element.542), channel_id=1, source_target_pairs={{16,0},{32,16},{48,32},{64,48},{80,64},{96,80},{112,96},{17,1},{33... | collective-permute-start | bytes 56 | tf_op jit(solution)/shard_map/ppermute | solution.py:17
  3.5 10.5 %collective-permute-start = (s32[1,2,2]{0,2,1:T(2,128)S(1)}, s32[1,2,2]{0,2,1:T(2,128)S(1)}, u32[]{:S(2)}, u32[]{:S(2)}) collective-permute-start(s32[1,2,2]{0,2,1:T(2,128)S(1)} %get-tuple-element.543), channel_id=1, source_target_pairs={{0,16},{16,32},{32,48},{48,64},{64,80},{80,96},{96,112},{1,17},{17... | collective-permute-start | bytes 56 | tf_op jit(solution)/shard_map/ppermute | solution.py:15
  8.5 26.6 %collective-permute-start.8 = (bf16[1,2,2,7,64,64]{5,3,4,2,1,0:T(8,128)(2,1)S(1)}, bf16[1,2,2,7,64,64]{5,3,4,2,1,0:T(8,128)(2,1)S(1)}, u32[]{:S(2)}, u32[]{:S(2)}) collective-permute-start(bf16[1,2,2,7,64,64]{5,3,4,2,1,0:T(8,128)(2,1)S(1)} %copy.218), channel_id=1, source_target_pairs={{0,16},{16,32},{32,48},{48,64},{64,80},{80,96},{96,112},{1,17},{17... | collective-permute-start | bytes 688136 | tf_op jit(solution)/shard_map/ppermute | solution.py:15
  11.2 24.6 %collective-permute-start.9 = (bf16[1,2,2,7,64,64]{5,3,4,2,1,0:T(8,128)(2,1)S(1)}, bf16[1,2,2,7,64,64]{5,3,4,2,1,0:T(8,128)(2,1)S(1)}, u32[]{:S(2)}, u32[]{:S(2)}) collective-permute-start(bf16[1,2,2,7,64,64]{5,3,4,2,1,0:T(8,128)(2,1)S(1)} %copy.219), channel_id=1, source_target_pairs={{16,0},{32,16},{48,32},{64,48},{80,64},{96,80},{112,96},{17,1},{33... | collective-permute-start | bytes 688136 | tf_op jit(solution)/shard_map/ppermute | solution.py:17
  15.2 6.8 %collective-permute-start.3 = (s32[4,1,2]{0,2,1:T(2,128)S(1)}, s32[4,1,2]{0,2,1:T(2,128)S(1)}, u32[]{:S(2)}, u32[]{:S(2)}) collective-permute-start(s32[4,1,2]{0,2,1:T(2,128)S(1)} %get-tuple-element.538), channel_id=1, source_target_pairs={{1,0},{2,1},{3,2},{4,3},{5,4},{6,5},{7,6},{8,7},{9,8},{10,9},{11,1... | collective-permute-start | bytes 104 | tf_op jit(solution)/shard_map/ppermute | solution.py:17
  20.1 6.4 %collective-permute-start.2 = (s32[4,1,2]{0,2,1:T(2,128)S(1)}, s32[4,1,2]{0,2,1:T(2,128)S(1)}, u32[]{:S(2)}, u32[]{:S(2)}) collective-permute-start(s32[4,1,2]{0,2,1:T(2,128)S(1)} %get-tuple-element.539), channel_id=1, source_target_pairs={{0,1},{1,2},{2,3},{3,4},{4,5},{5,6},{6,7},{7,8},{8,9},{9,10},{10,1... | collective-permute-start | bytes 104 | tf_op jit(solution)/shard_map/ppermute | solution.py:15
  28.1 13.8 %collective-permute-start.4 = (s32[1,2,2,7]{3,2,1,0:T(2,128)S(1)}, s32[1,2,2,7]{3,2,1,0:T(2,128)S(1)}, u32[]{:S(2)}, u32[]{:S(2)}) collective-permute-start(s32[1,2,2,7]{3,2,1,0:T(2,128)S(1)} %get-tuple-element.534), channel_id=1, source_target_pairs={{0,16},{16,32},{32,48},{48,64},{64,80},{80,96},{96,112},{1,17},{17... | collective-permute-start | bytes 344 | tf_op jit(solution)/shard_map/ppermute | solution.py:15
  33.2 8.7 %collective-permute-start.5 = (s32[1,2,2,7]{3,2,1,0:T(2,128)S(1)}, s32[1,2,2,7]{3,2,1,0:T(2,128)S(1)}, u32[]{:S(2)}, u32[]{:S(2)}) collective-permute-start(s32[1,2,2,7]{3,2,1,0:T(2,128)S(1)} %get-tuple-element.535), channel_id=1, source_target_pairs={{16,0},{32,16},{48,32},{64,48},{80,64},{96,80},{112,96},{17,1},{33... | collective-permute-start | bytes 344 | tf_op jit(solution)/shard_map/ppermute | solution.py:17
  35.9 13.5 %copy-start.10 = (s32[2,2,2,6]{3,2,1,0:T(2,128)S(1)}, s32[2,2,2,6]{3,2,1,0:T(2,128)}, u32[]{:S(2)}) copy-start(s32[2,2,2,6]{3,2,1,0:T(2,128)} %param.89) | copy-start | bytes 580
  36.6 27.8 %collective-permute-start.11 = (bf16[4,1,2,7,64,64]{5,4,3,2,1,0:T(8,128)(2,1)S(1)}, bf16[4,1,2,7,64,64]{5,4,3,2,1,0:T(8,128)(2,1)S(1)}, u32[]{:S(2)}, u32[]{:S(2)}) collective-permute-start(bf16[4,1,2,7,64,64]{5,4,3,2,1,0:T(8,128)(2,1)S(1)} %copy.143), channel_id=1, source_target_pairs={{1,0},{2,1},{3,2},{4,3},{5,4},{6,5},{7,6},{8,7},{9,8},{10,9},{11,1... | collective-permute-start | bytes 1376264 | tf_op jit(solution)/shard_map/ppermute | solution.py:17
  38.5 26.5 %collective-permute-start.10 = (bf16[4,1,2,7,64,64]{5,4,3,2,1,0:T(8,128)(2,1)S(1)}, bf16[4,1,2,7,64,64]{5,4,3,2,1,0:T(8,128)(2,1)S(1)}, u32[]{:S(2)}, u32[]{:S(2)}) collective-permute-start(bf16[4,1,2,7,64,64]{5,4,3,2,1,0:T(8,128)(2,1)S(1)} %copy.142), channel_id=1, source_target_pairs={{0,1},{1,2},{2,3},{3,4},{4,5},{5,6},{6,7},{7,8},{8,9},{9,10},{10,1... | collective-permute-start | bytes 1376264 | tf_op jit(solution)/shard_map/ppermute | solution.py:15
  42.0 22.4 %collective-permute-start.6 = (s32[4,1,2,7]{3,2,1,0:T(2,128)S(1)}, s32[4,1,2,7]{3,2,1,0:T(2,128)S(1)}, u32[]{:S(2)}, u32[]{:S(2)}) collective-permute-start(s32[4,1,2,7]{3,2,1,0:T(2,128)S(1)} %get-tuple-element.530), channel_id=1, source_target_pairs={{0,1},{1,2},{2,3},{3,4},{4,5},{5,6},{6,7},{7,8},{8,9},{9,10},{10,1... | collective-permute-start | bytes 680 | tf_op jit(solution)/shard_map/ppermute | solution.py:15
  43.9 20.5 %collective-permute-start.7 = (s32[4,1,2,7]{3,2,1,0:T(2,128)S(1)}, s32[4,1,2,7]{3,2,1,0:T(2,128)S(1)}, u32[]{:S(2)}, u32[]{:S(2)}) collective-permute-start(s32[4,1,2,7]{3,2,1,0:T(2,128)S(1)} %get-tuple-element.531), channel_id=1, source_target_pairs={{1,0},{2,1},{3,2},{4,3},{5,4},{6,5},{7,6},{8,7},{9,8},{10,9},{11,1... | collective-permute-start | bytes 680 | tf_op jit(solution)/shard_map/ppermute | solution.py:17
  78.4 1.2 copy-start.9
  88.0 1.6 copy-start.8
  109.9 2.2 copy-start.7
  111.8 1.2 copy-start.6
  111.8 1.4 copy-start.5
  111.9 1.6 copy-start.4
  112.2 1.6 copy-start.3
  112.9 1.3 copy-start.2
  114.5 8.8 %copy-start = (f32[3,3,7,7,64,64]{5,4,3,2,0,1:T(8,128)}, f32[3,3,7,7,64,64]{5,4,3,2,0,1:T(8,128)S(1)}, u32[]{:S(2)}) copy-start(f32[3,3,7,7,64,64]{5,4,3,2,0,1:T(8,128)S(1)} %fusion.19) | copy-start | bytes 21676036
  123.3 106.6 %collective-permute-start.12 = (f32[3,7,7,64,64]{4,3,2,1,0:T(8,128)}, f32[3,7,7,64,64]{4,3,2,1,0:T(8,128)S(1)}, u32[]{:S(2)}, u32[]{:S(2)}) collective-permute-start(f32[3,7,7,64,64]{4,3,2,1,0:T(8,128)} %get-tuple-element.505), channel_id=1, source_target_pairs={{1,0},{2,1},{3,2},{4,3},{5,4},{6,5},{7,6},{8,7},{9,8},{10,9},{11,1... | collective-permute-start | bytes 7225352 | tf_op jit(solution)/shard_map/ppermute | solution.py:27
  125.2 108.7 %collective-permute-start.13 = (f32[3,7,7,64,64]{4,3,2,1,0:T(8,128)}, f32[3,7,7,64,64]{4,3,2,1,0:T(8,128)}, u32[]{:S(2)}, u32[]{:S(2)}) collective-permute-start(f32[3,7,7,64,64]{4,3,2,1,0:T(8,128)} %get-tuple-element.506), channel_id=1, source_target_pairs={{0,1},{1,2},{2,3},{3,4},{4,5},{5,6},{6,7},{7,8},{8,9},{9,10},{10,1... | collective-permute-start | bytes 7225352 | tf_op jit(solution)/shard_map/ppermute | solution.py:27
  240.2 14.9 %collective-permute-start.14 = (bf16[1,7,7,64,64]{4,3,2,1,0:T(8,128)(2,1)S(1)}, bf16[1,7,7,64,64]{4,3,2,1,0:T(8,128)(2,1)S(1)}, u32[]{:S(2)}, u32[]{:S(2)}) collective-permute-start(bf16[1,7,7,64,64]{4,3,2,1,0:T(8,128)(2,1)S(1)} %get-tuple-element.524), channel_id=1, source_target_pairs={{16,0},{32,16},{48,32},{64,48},{80,64},{96,80},{112,96},{17,1},{33... | collective-permute-start | bytes 1204232 | tf_op jit(solution)/shard_map/ppermute | solution.py:27
  244.1 11.9 %collective-permute-start.15 = (bf16[1,7,7,64,64]{4,3,2,1,0:T(8,128)(2,1)S(1)}, bf16[1,7,7,64,64]{4,3,2,1,0:T(8,128)(2,1)S(1)}, u32[]{:S(2)}, u32[]{:S(2)}) collective-permute-start(bf16[1,7,7,64,64]{4,3,2,1,0:T(8,128)(2,1)S(1)} %get-tuple-element.525), channel_id=1, source_target_pairs={{0,16},{16,32},{32,48},{48,64},{64,80},{80,96},{96,112},{1,17},{17... | collective-permute-start | bytes 1204232 | tf_op jit(solution)/shard_map/ppermute | solution.py:27
where the time goes:
time: 259 us; the launch traced here: 257 us
  waiting for transfers between devices  134 us (52%)
  starting transfers between devices  48.7 us (19%)
  local copies, waits for them, and re-layouts  44.5 us (17%)
  other arithmetic  16 us (6%)
  matrix products  13.4 us (5%)
    ppermute x4, waiting for transfers between devices, from_behind(): return lax.ppermute(value, axis, pairs)  114 us
    ppermute x6, waiting for transfers between devices, extended_2(): lax.ppermute(tail, axis, [(i, (i + 1) % count) for i in range(ends)])  19.3 us
    ppermute x6, starting transfers between devices, extended_2(): lax.ppermute(head, axis, [((i + 1) % count, i) for i in range(ends)])  18.7 us
    ppermute x6, starting transfers between devices, extended_2(): lax.ppermute(tail, axis, [(i, (i + 1) % count) for i in range(ends)])  18.1 us
    another operation x7, local copies, waits for them, and re-layouts  13.1 us
    ppermute x4, starting transfers between devices, from_behind(): return lax.ppermute(value, axis, pairs)  11.9 us
    unnamed x27, local copies, waits for them, and re-layouts  7.34 us
    another operation x1, other arithmetic  6.2 us
  transfers between devices with their start and end apart: 16, of which 6 were waited for; matrix products, arithmetic and copies ran while one was open for 3% of the time, Pallas kernels for 0%

commit v1 on v0

v1 whole, which is shorter than its diff:
```python
import functools

import jax
import jax.numpy as jnp
from jax import lax
from jax.experimental import pallas as pl
from jax.experimental.pallas import tpu as pltpu
from jax.sharding import PartitionSpec as P

MESH = pl.DeviceIdType.MESH
F32 = jnp.float32
BF16 = jnp.bfloat16

CORNERS = ((-1, -1), (-1, 1), (1, -1), (1, 1))
FACES = ((-1, 0), (1, 0), (0, -1), (0, 1))
NOWHERE = -1000000

EVENS = ((0, 0), (-1, 0), (1, 0), (-2, 0), (2, 0), (0, -2), (0, 2))
ODDS = ((0, -1), (0, 1), (-1, -1), (-1, 1), (1, -1), (1, 1), None)
PAIRS = tuple(zip(EVENS, ODDS))


def corner(sx, sy):
    return (2 if sx > 0 else 0) + (1 if sy > 0 else 0)


def element_tiles(sx, sy):
    return (((0, 0), (sx, sy)), ((sx, 0), (0, sy)), ((-sx, 0), (0, -sy)))


def image_tiles(sx, sy):
    return element_tiles(sx, sy) + (((2 * sx, 0), (sx, -sy)), ((0, 2 * sy), (-sx, sy)))


def slots(sx, sy):
    return (2 if sx < 0 else 1), (4 if sy < 0 else 3), (1 if sx < 0 else 2), (3 if sy < 0 else 4)


def add(u, v):
    return (u[0] + v[0], u[1] + v[1])


def dot(a, b):
    return jnp.dot(a, b, preferred_element_type=F32)


def kernel(
    nx, ny, a_hbm, p_hbm, agg, links, out,
    a_v, p_v, tab, gtab, part, tiles, gx, gy, mats, im, ptg, ptd, imw,
    face_out, face_in, diag_out, diag_in, acc,
    ld_sem, agg_s, agg_r, early_s, early_r, late_s, late_r, face_s, face_r, diag_s, diag_r,
):
    mx, my = lax.axis_index("sx"), lax.axis_index("sy")
    par = lax.rem(my, 2)

    def device(dx, dy):
        return (lax.rem(mx + dx + nx, nx), lax.rem(my + dy + ny, ny))

    def box_id(t):
        return (mx + t[0]) * ny + my + t[1]

    barrier = pltpu.get_barrier_semaphore()
    for d in FACES + CORNERS:
        pl.semaphore_signal(barrier, inc=1, device_id=device(*d), device_id_type=MESH)
    load_p = pltpu.make_async_copy(p_hbm, p_v, ld_sem.at[0])
    load_a = pltpu.make_async_copy(a_hbm, a_v, ld_sem.at[1])
    load_p.start()
    load_a.start()

    for x in range(2):
        for y in range(2):
            for z in range(2):
                tab[4 * x + 2 * y + z, :] = jnp.full((128,), agg[x, y, z], jnp.int32)

    half = (lax.broadcasted_iota(jnp.int32, (1, 128), 1) >= 64).astype(jnp.int32)
    even_row = half == par
    even = jnp.broadcast_to(((lax.broadcasted_iota(jnp.int32, (128, 128), 1) >= 64).astype(jnp.int32)) == par, (128, 128))

    def lane_ids(pair):
        return jnp.where(even_row, box_id(pair[0]), box_id(pair[1]))

    def doubled(x, y, z, m):
        block = p_v[x, y, z, m].astype(F32)
        return jnp.concatenate([block, block], axis=1)

    def picked(ids, target):
        return (ids == target).astype(F32)

    load_p.wait()
    for c, (sx, sy) in enumerate(CORNERS):
        x, y = (sx + 1) // 2, (sy + 1) // 2
        ix, iy, ox, oy = slots(sx, sy)
        ids = [lane_ids(pair) for pair in element_tiles(sx, sy)]
        for z in range(2):
            mz = 6 if z == 0 else 5
            total = [None, None, None]
            for m, (ex, ey, ez) in ((0, (x, y, z)), (mz, (x, y, 1 - z)), (ix, (1 - x, y, z)), (iy, (x, 1 - y, z))):
                target = agg[ex, ey, ez]
                if m > 0:
                    target = jnp.where(links[x, y, z, m - 1] == 1, target, NOWHERE)
                block = doubled(x, y, z, m)
                for t in range(3):
                    if t == 2 and m in (0, mz):
                        continue
                    term = block * picked(ids[t], target)
                    total[t] = term if total[t] is None else total[t] + term
            tiles[c, 2, 64 * z : 64 * z + 64, :] = total[2].astype(BF16)
            part[2 * c + z, 0] = total[0]
            part[2 * c + z, 1] = total[1]

    pl.semaphore_wait(barrier, 8)

    agg_copies = []
    for d, (dx, dy) in enumerate(FACES):
        agg_copies.append(
            pltpu.make_async_remote_copy(
                src_ref=tab, dst_ref=gtab.at[d], send_sem=agg_s.at[d], recv_sem=agg_r.at[d],
                device_id=device(-dx, -dy), device_id_type=MESH,
            )
        )
        agg_copies[-1].start()

    def ghost_copy(c, along_y, early):
        sx, sy = CORNERS[c]
        k = 4 + c if along_y else c
        src = tiles.at[corner(sx, -sy) if along_y else corner(-sx, sy)]
        dst = (gy if along_y else gx).at[c]
        part_of = pl.ds(2, 1) if early else pl.ds(0, 2)
        return pltpu.make_async_remote_copy(
            src_ref=src.at[part_of], dst_ref=dst.at[part_of],
            send_sem=(early_s if early else late_s).at[k], recv_sem=(early_r if early else late_r).at[k],
            device_id=device(0, -sy) if along_y else device(-sx, 0), device_id_type=MESH,
        )

    early_copies = {}
    for along_y in (True, False):
        for c in range(4):
            early_copies[along_y, c] = ghost_copy(c, along_y, True)
            early_copies[along_y, c].start()

    load_a.wait()
    for c, (sx, sy) in enumerate(CORNERS):
        x, y = (sx + 1) // 2, (sy + 1) // 2

        def block(z, m):
            value = a_v[x, y, z, m]
            if m == 0:
                return value
            return (value.astype(F32) * links[x, y, z, m - 1].astype(F32)).astype(BF16)

        mats[c, 0, 0:64, :] = jnp.concatenate([block(0, 0), block(0, 6)], axis=1)
        mats[c, 0, 64:128, :] = jnp.concatenate([block(1, 5), block(1, 0)], axis=1)
        zero = jnp.zeros((64, 64), BF16)
        for k, m in enumerate(slots(sx, sy)):
            mats[c, k + 1, 0:64, :] = jnp.concatenate([block(0, m), zero], axis=1)
            mats[c, k + 1, 64:128, :] = jnp.concatenate([zero, block(1, m)], axis=1)

    for copy in agg_copies:
        copy.wait_recv()
    late_copies = {}
    for c, (sx, sy) in enumerate(CORNERS):
        x, y = (sx + 1) // 2, (sy + 1) // 2
        ix, iy, ox, oy = slots(sx, sy)
        ids = [lane_ids(pair) for pair in element_tiles(sx, sy)]
        for z in range(2):
            row_x = gtab[FACES.index((sx, 0)), pl.ds(4 * (1 - x) + 2 * y + z, 1), :]
            row_y = gtab[FACES.index((0, sy)), pl.ds(4 * x + 2 * (1 - y) + z, 1), :]
            row_x = jnp.where(links[x, y, z, ox - 1] == 1, row_x, NOWHERE)
            row_y = jnp.where(links[x, y, z, oy - 1] == 1, row_y, NOWHERE)
            block_x, block_y = doubled(x, y, z, ox), doubled(x, y, z, oy)
            for t in range(2):
                total = part[2 * c + z, t] + block_x * picked(ids[t], row_x) + block_y * picked(ids[t], row_y)
                tiles[c, t, 64 * z : 64 * z + 64, :] = total.astype(BF16)
        for along_y, to in ((True, corner(sx, -sy)), (False, corner(-sx, sy))):
            late_copies[along_y, to] = ghost_copy(to, along_y, False)
            late_copies[along_y, to].start()

    top = jnp.full((64, 128), par, jnp.int32) == 0
    for c, (sx, sy) in enumerate(CORNERS):
        blocks = {}
        for t, pair in enumerate(element_tiles(sx, sy)):
            turned = tiles[c, t].astype(F32).T
            blocks[pair[0]] = jnp.where(top, turned[0:64], turned[64:128]).astype(BF16)
            blocks[pair[1]] = jnp.where(top, turned[64:128], turned[0:64]).astype(BF16)
        ptd[c] = blocks[sx, sy]
        for r, offset in enumerate(FACES + ((0, 0),)):
            ptg[64 * r : 64 * r + 64, 128 * c : 128 * c + 128] = blocks[offset]

    def product(mat, ref, c):
        rows = dot(mat, jnp.concatenate([ref[c, 0], ref[c, 1], ref[c, 2]], axis=1))
        return rows[:, 0:128], rows[:, 128:256], rows[:, 256:384]

    nothing = jnp.zeros((128, 128), F32)
    for c, (sx, sy) in enumerate(CORNERS):
        s0, s1, s2 = product(mats[c, 0], tiles, c)
        x0, x1, x2 = product(mats[c, 1], tiles, corner(-sx, sy))
        y0, y1, y2 = product(mats[c, 2], tiles, corner(sx, -sy))
        im[c, 0] = s0 + jnp.where(even, x0 + y0, nothing)
        im[c, 1] = s1 + jnp.where(even, x2 + y1, x1 + y2)
        im[c, 2] = s2 + jnp.where(even, x1 + y2, x2 + y1)
        im[c, 3] = jnp.where(even, nothing, y0)
        im[c, 4] = jnp.where(even, nothing, x0)

    for jx in range(7):
        for jy in range(7):
            if abs(jx - 3) + abs(jy - 3) > 3:
                out[0, 0, jx, jy] = jnp.zeros((64, 64), BF16)

    for copy in late_copies.values():
        pass
    diag_copies, face_copies = {}, {}
    for c, (sx, sy) in enumerate(CORNERS):
        early_copies[False, c].wait_recv()
        late_copies[False, c].wait_recv()
        early_copies[True, c].wait_recv()
        late_copies[True, c].wait_recv()
        x0, x1, x2 = product(mats[c, 3], gx, c)
        y0, y1, y2 = product(mats[c, 4], gy, c)
        image = [
            (im[c, 0] + x1 + y1).astype(BF16),
            (im[c, 1] + x0 + y0).astype(BF16),
            im[c, 2].astype(BF16),
            (im[c, 3] + x2).astype(BF16),
            (im[c, 4] + y2).astype(BF16),
        ]
        diag_out[c] = dot(ptd[c], jnp.concatenate(image, axis=1)).astype(BF16)
        to = corner(-sx, -sy)
        diag_copies[to] = pltpu.make_async_remote_copy(
            src_ref=diag_out.at[c], dst_ref=diag_in.at[to], send_sem=diag_s.at[to], recv_sem=diag_r.at[to],
            device_id=device(sx, sy), device_id_type=MESH,
        )
        diag_copies[to].start()
        names = image_tiles(sx, sy)
        at_even = {pair[0]: i for i, pair in enumerate(names)}
        at_odd = {pair[1]: i for i, pair in enumerate(names)}
        for g, (e, o) in enumerate(PAIRS):
            left = image[at_even[e]].astype(F32) if e in at_even else nothing
            right = image[at_odd[o]].astype(F32) if o in at_odd else nothing
            imw[128 * c : 128 * c + 128, 128 * g : 128 * g + 128] = jnp.where(even, left, right).astype(BF16)

    def send_face(d):
        dx, dy = FACES[d]
        to = FACES.index((-dx, -dy))
        face_copies[to] = pltpu.make_async_remote_copy(
            src_ref=face_out.at[d], dst_ref=face_in.at[to], send_sem=face_s.at[to], recv_sem=face_r.at[to],
            device_id=device(dx, dy), device_id_type=MESH,
        )
        face_copies[to].start()

    wide = imw[...]
    for first in (2, 0):
        rows = dot(ptg[64 * first : 64 * first + 128, :], wide).astype(BF16)
        for d in (first, first + 1):
            face_out[d] = rows[64 * (d - first) : 64 * (d - first) + 64]
            send_face(d)

    offsets = [(dx, dy) for dx in range(-3, 4) for dy in range(-3, 4) if abs(dx) + abs(dy) <= 3]
    at = {offset: i for i, offset in enumerate(offsets)}
    own = dot(ptg[256:320, :], wide)
    for offset in offsets:
        acc[at[offset]] = jnp.zeros((64, 128), F32)
    for g, pair in enumerate(PAIRS):
        for offset in pair:
            if offset is not None:
                acc[at[offset]] = own[:, 128 * g : 128 * g + 128]

    for d in (0, 1):
        face_copies[d].wait_recv()
        for g, pair in enumerate(PAIRS):
            tile = face_in[d, :, 128 * g : 128 * g + 128].astype(F32)
            for offset in pair:
                if offset is not None:
                    acc[at[add(offset, FACES[d])]] += tile
    for c, (sx, sy) in enumerate(CORNERS):
        diag_copies[c].wait_recv()
        for g, pair in enumerate(image_tiles(-sx, -sy)):
            tile = diag_in[c, :, 128 * g : 128 * g + 128].astype(F32)
            for offset in pair:
                acc[at[add(offset, (sx, sy))]] += tile
    for d in (2, 3):
        face_copies[d].wait_recv()
        for g, pair in enumerate(PAIRS):
            tile = face_in[d, :, 128 * g : 128 * g + 128].astype(F32)
            for offset in pair:
                if offset is not None:
                    acc[at[add(offset, FACES[d])]] += tile

    for offset in offsets:
        value = acc[at[offset]]
        other = pltpu.roll(value, 64, 1)
        first = top if offset[1] % 2 == 0 else jnp.logical_not(top)
        out[0, 0, offset[0] + 3, offset[1] + 3] = jnp.where(first, value, other)[:, 0:64].astype(BF16)

    for copies in (agg_copies, early_copies.values(), late_copies.values(), diag_copies.values(), face_copies.values()):
        for copy in copies:
            copy.wait_send()


def per_device(fine_matrix, prolongator, aggregate, face_links):
    nx, ny = lax.axis_size("sx"), lax.axis_size("sy")
    dma = pltpu.SemaphoreType.DMA
    return pl.pallas_call(
        functools.partial(kernel, nx, ny),
        out_shape=jax.ShapeDtypeStruct((1, 1, 7, 7, 64, 64), BF16),
        in_specs=[
            pl.BlockSpec(memory_space=pl.ANY),
            pl.BlockSpec(memory_space=pl.ANY),
            pl.BlockSpec(memory_space=pltpu.SMEM),
            pl.BlockSpec(memory_space=pltpu.SMEM),
        ],
        out_specs=pl.BlockSpec(memory_space=pltpu.VMEM),
        scratch_shapes=[
            pltpu.VMEM((2, 2, 2, 7, 64, 64), BF16),
            pltpu.VMEM((2, 2, 2, 7, 64, 64), BF16),
            pltpu.VMEM((8, 128), jnp.int32),
            pltpu.VMEM((4, 8, 128), jnp.int32),
            pltpu.VMEM((8, 2, 64, 128), F32),
            pltpu.VMEM((4, 3, 128, 128), BF16),
            pltpu.VMEM((4, 3, 128, 128), BF16),
            pltpu.VMEM((4, 3, 128, 128), BF16),
            pltpu.VMEM((4, 5, 128, 128), BF16),
            pltpu.VMEM((4, 5, 128, 128), F32),
            pltpu.VMEM((320, 512), BF16),
            pltpu.VMEM((4, 64, 128), BF16),
            pltpu.VMEM((512, 896), BF16),
            pltpu.VMEM((4, 64, 896), BF16),
            pltpu.VMEM((4, 64, 896), BF16),
            pltpu.VMEM((4, 64, 640), BF16),
            pltpu.VMEM((4, 64, 640), BF16),
            pltpu.VMEM((25, 64, 128), F32),
            dma((2,)),
            dma((4,)),
            dma((4,)),
            dma((8,)),
            dma((8,)),
            dma((8,)),
            dma((8,)),
            dma((4,)),
            dma((4,)),
            dma((4,)),
            dma((4,)),
        ],
        compiler_params=pltpu.CompilerParams(
            collective_id=0, has_side_effects=True, vmem_limit_bytes=32 * 1024 * 1024
        ),
        name="galerkin",
    )(fine_matrix, prolongator, aggregate, face_links)


def solution(mesh):
    return jax.shard_map(
        per_device,
        mesh=mesh,
        in_specs=(
            P("sx", "sy", None, None, None, None),
            P("sx", "sy", None, None, None, None),
            P("sx", "sy", None),
            P("sx", "sy", None, None),
        ),
        out_specs=P("sx", "sy", None, None, None, None),
        check_vma=False,
    )
```

time: 259 us -> 31.1 us (0.12)
  the two profiles are of different devices: /device:TPU:39 before, /device:TPU:0 now
where the time goes in v1:
time: 31.1 us; the launch traced here: 30.9 us
  Pallas kernels  26.2 us (84%)
  local copies, waits for them, and re-layouts  4.61 us (15%)
    pallas_call x1, Pallas kernels, per_device(): pl.pallas_call(functools.partial(kernel, nx, ny), out_shape=jax.ShapeDtyp...  26.2 us
    unnamed x9, local copies, waits for them, and re-layouts  4.61 us

profile of v1, /device:TPU:0, one launch (start us, length us, event | category | flops | bytes accessed | tf_op | source)
XLA Modules:
  0.0 30.9 jit_solution(671909127025208195)
XLA Ops:
  0.0 0.0 copy-start
  0.0 1.2 %copy-done = bf16[2,2,2,7,64,64]{5,4,3,2,1,0:T(8,128)(2,1)S(1)} copy-done((bf16[2,2,2,7,64,64]{5,4,3,2,1,0:T(8,128)(2,1)S(1)}, bf16[2,2,2,7,64,64]{5,4,3,2,1,0:T(8,128)(2,1)}, u32[]{:S(2)}) %copy-start) | copy-done | bytes 458776
  1.2 0.0 copy-start.1
  1.2 1.2 %copy-done.1 = bf16[2,2,2,7,64,64]{5,4,3,2,1,0:T(8,128)(2,1)S(1)} copy-done((bf16[2,2,2,7,64,64]{5,4,3,2,1,0:T(8,128)(2,1)S(1)}, bf16[2,2,2,7,64,64]{5,4,3,2,1,0:T(8,128)(2,1)}, u32[]{:S(2)}) %copy-start.1) | copy-done | bytes 458776
  2.4 0.0 copy-start.2
  2.4 0.7 %copy-done.2 = s32[2,2,2,6]{3,2,1,0:T(2,128)S(1)} copy-done((s32[2,2,2,6]{3,2,1,0:T(2,128)S(1)}, s32[2,2,2,6]{3,2,1,0:T(2,128)}, u32[]{:S(2)}) %copy-start.2) | copy-done | bytes 216
  3.0 0.0 copy-start.3
  3.0 0.7 %copy-done.3 = s32[2,2,2]{2,1,0:T(2,128)S(1)} copy-done((s32[2,2,2]{2,1,0:T(2,128)S(1)}, s32[2,2,2]{2,1,0:T(2,128)}, u32[]{:S(2)}) %copy-start.3) | copy-done | bytes 56
  3.7 26.2 %galerkin.1 = bf16[1,1,7,7,64,64]{5,4,3,2,1,0:T(8,128)(2,1)S(1)} custom-call(bf16[2,2,2,7,64,64]{5,4,3,2,1,0:T(8,128)(2,1)S(1)} %copy-done, bf16[2,2,2,7,64,64]{5,4,3,2,1,0:T(8,128)(2,1)S(1)} %copy-done.1, s32[2,2,2]{2,1,0:T(2,128)S(1)} %copy-done.3, s32[2,2,2,6]{3,2,1,0:T(2,128)S(1)} %copy-done.2), custom_call_target="tpu_custom_call" | custom-call | tf_op jit(solution)/shard_map/galerkin/pallas_call | solution.py:302
  30.0 0.9 %copy.6 = bf16[1,1,7,7,64,64]{5,4,3,2,1,0:T(8,128)(2,1)} copy(bf16[1,1,7,7,64,64]{5,4,3,2,1,0:T(8,128)(2,1)S(1)} %galerkin.1) | data formatting | bytes 802816
Async XLA Ops:
  0.0 1.2 %copy-start = (bf16[2,2,2,7,64,64]{5,4,3,2,1,0:T(8,128)(2,1)S(1)}, bf16[2,2,2,7,64,64]{5,4,3,2,1,0:T(8,128)(2,1)}, u32[]{:S(2)}) copy-start(bf16[2,2,2,7,64,64]{5,4,3,2,1,0:T(8,128)(2,1)} %a_hbm.1) | copy-start | bytes 1376260
  1.2 1.2 %copy-start.1 = (bf16[2,2,2,7,64,64]{5,4,3,2,1,0:T(8,128)(2,1)S(1)}, bf16[2,2,2,7,64,64]{5,4,3,2,1,0:T(8,128)(2,1)}, u32[]{:S(2)}) copy-start(bf16[2,2,2,7,64,64]{5,4,3,2,1,0:T(8,128)(2,1)} %p_hbm.1) | copy-start | bytes 1376260
  2.4 0.7 %copy-start.2 = (s32[2,2,2,6]{3,2,1,0:T(2,128)S(1)}, s32[2,2,2,6]{3,2,1,0:T(2,128)}, u32[]{:S(2)}) copy-start(s32[2,2,2,6]{3,2,1,0:T(2,128)} %links.1) | copy-start | bytes 580
  3.0 0.7 %copy-start.3 = (s32[2,2,2]{2,1,0:T(2,128)S(1)}, s32[2,2,2]{2,1,0:T(2,128)}, u32[]{:S(2)}) copy-start(s32[2,2,2]{2,1,0:T(2,128)} %agg.1) | copy-start | bytes 100

commit v2 on v1

v2 whole, which is shorter than its diff:
```python
import functools

import jax
import jax.numpy as jnp
from jax import lax
from jax.experimental import pallas as pl
from jax.experimental.pallas import tpu as pltpu
from jax.sharding import PartitionSpec as P

MESH = pl.DeviceIdType.MESH
F32 = jnp.float32
BF16 = jnp.bfloat16

CORNERS = ((-1, -1), (-1, 1), (1, -1), (1, 1))
FACES = ((-1, 0), (1, 0), (0, -1), (0, 1))
DIRECTIONS = FACES + CORNERS
NOWHERE = -1000000
FACTS = 6

EVENS = ((0, 0), (-1, 0), (1, 0), (-2, 0), (2, 0), (0, -2), (0, 2))
ODDS = ((0, -1), (0, 1), (-1, -1), (-1, 1), (1, -1), (1, 1), None)
PAIRS = tuple(zip(EVENS, ODDS))


def corner(sx, sy):
    return (2 if sx > 0 else 0) + (1 if sy > 0 else 0)


def element_tiles(sx, sy):
    return (((0, 0), (sx, sy)), ((sx, 0), (0, sy)), ((-sx, 0), (0, -sy)))


def image_tiles(sx, sy):
    return element_tiles(sx, sy) + (((2 * sx, 0), (sx, -sy)), ((0, 2 * sy), (-sx, sy)))


def slots(sx, sy):
    return (2 if sx < 0 else 1), (4 if sy < 0 else 3), (1 if sx < 0 else 2), (3 if sy < 0 else 4)


def add(u, v):
    return (u[0] + v[0], u[1] + v[1])


def dot(a, b):
    return jnp.dot(a, b, preferred_element_type=F32)


def kernel(
    nx, ny, a_hbm, p_hbm, agg_hbm, links_hbm, out,
    a_v, p_v, agg, links, facts, facts_in, raw, raw_x, raw_y, tiles, tiles_x, tiles_y, mats, im, ptg, ptd, imw,
    face_out, face_in, first_out, first_in, rest_out, rest_in, acc,
    scalar_sem, p_sem, a_sem, facts_s, facts_r, raw_s, raw_r, face_s, face_r, first_s, first_r, rest_s, rest_r,
):
    mx, my = lax.axis_index("sx"), lax.axis_index("sy")
    par = lax.rem(my, 2)

    def device(dx, dy):
        return (lax.rem(mx + dx + nx, nx), lax.rem(my + dy + ny, ny))

    inside = {(-1, 0): mx > 0, (1, 0): mx < nx - 1, (0, -1): my > 0, (0, 1): my < ny - 1}
    for sx, sy in CORNERS:
        inside[sx, sy] = jnp.logical_and(inside[sx, 0], inside[0, sy])

    def when(d, action):
        pl.when(inside[d])(action)

    def remote(src, dst, sems, k, d):
        return pltpu.make_async_remote_copy(
            src_ref=src, dst_ref=dst, send_sem=sems[0].at[k], recv_sem=sems[1].at[k],
            device_id=device(*d), device_id_type=MESH,
        )

    barrier = pltpu.get_barrier_semaphore()
    for d in DIRECTIONS:
        when(d, lambda: pl.semaphore_signal(barrier, inc=1, device_id=device(*d), device_id_type=MESH))
    scalar_loads = (
        pltpu.make_async_copy(agg_hbm, agg, scalar_sem.at[0]),
        pltpu.make_async_copy(links_hbm, links, scalar_sem.at[1]),
    )
    p_loads, a_loads = [], []
    for c, (sx, sy) in enumerate(CORNERS):
        x, y = (sx + 1) // 2, (sy + 1) // 2
        p_loads.append(pltpu.make_async_copy(p_hbm.at[x, y], p_v.at[x, y], p_sem.at[c]))
        a_loads.append(pltpu.make_async_copy(a_hbm.at[x, y], a_v.at[x, y], a_sem.at[c]))
    for copy in (*scalar_loads, *p_loads, *a_loads):
        copy.start()

    left = lax.broadcasted_iota(jnp.int32, (1, 128), 1) < 64
    even_row = (lax.broadcasted_iota(jnp.int32, (1, 128), 1) >= 64).astype(jnp.int32) == par
    even = (lax.broadcasted_iota(jnp.int32, (128, 128), 1) >= 64).astype(jnp.int32) == par
    top = jnp.full((64, 128), par, jnp.int32) == 0

    for side in FACES:

        @pl.when(jnp.logical_not(inside[side]))
        def _():
            for c, (sx, sy) in enumerate(CORNERS):
                if side == (sx, 0):
                    raw_x[c] = jnp.zeros((3, 128, 128), BF16)
                if side == (0, sy):
                    raw_y[c] = jnp.zeros((3, 128, 128), BF16)

    def place(x, y, z, fact):
        return FACTS * (4 * x + 2 * y + z) + fact

    for copy in scalar_loads:
        copy.wait()
    for c, (sx, sy) in enumerate(CORNERS):
        x, y = (sx + 1) // 2, (sy + 1) // 2
        ix, iy, ox, oy = slots(sx, sy)
        for z in range(2):
            mz = 6 if z == 0 else 5
            mine = agg[x, y, z]
            facts[place(x, y, z, 0)] = mine
            for fact, m, target in (
                (1, mz, agg[x, y, 1 - z]), (2, ix, agg[1 - x, y, z]), (3, iy, agg[x, 1 - y, z]), (4, ox, mine), (5, oy, mine)
            ):
                facts[place(x, y, z, fact)] = jnp.where(links[x, y, z, m - 1] == 1, target, NOWHERE)

    for c, (sx, sy) in enumerate(CORNERS):
        x, y = (sx + 1) // 2, (sy + 1) // 2
        ix, iy, ox, oy = slots(sx, sy)
        p_loads[c].wait()
        for z in range(2):
            for j, (m, n) in enumerate(((0, 6 if z == 0 else 5), (ix, iy), (ox, oy))):
                raw[c, j, 64 * z : 64 * z + 64, :] = jnp.concatenate([p_v[x, y, z, m], p_v[x, y, z, n]], axis=1)

    pl.semaphore_wait(barrier, sum(there.astype(jnp.int32) for there in inside.values()))

    facts_copies = {}
    for k, (dx, dy) in enumerate(DIRECTIONS):
        facts_copies[dx, dy] = remote(facts, facts_in.at[k], (facts_s, facts_r), k, (-dx, -dy))
        when((-dx, -dy), facts_copies[dx, dy].start)
    copies_x, copies_y = [], []
    for c, (sx, sy) in enumerate(CORNERS):
        copies_x.append(remote(raw.at[corner(-sx, sy)], raw_x.at[c], (raw_s, raw_r), c, (-sx, 0)))
        copies_y.append(remote(raw.at[corner(sx, -sy)], raw_y.at[c], (raw_s, raw_r), 4 + c, (0, -sy)))
    for c, (sx, sy) in enumerate(CORNERS):
        when((0, -sy), copies_y[c].start)
    for c, (sx, sy) in enumerate(CORNERS):
        when((-sx, 0), copies_x[c].start)

    for c, (sx, sy) in enumerate(CORNERS):
        x, y = (sx + 1) // 2, (sy + 1) // 2
        a_loads[c].wait()

        def block(z, m):
            value = a_v[x, y, z, m]
            if m == 0:
                return value
            return (value.astype(F32) * links[x, y, z, m - 1].astype(F32)).astype(BF16)

        mats[c, 0, 0:64, :] = jnp.concatenate([block(0, 0), block(0, 6)], axis=1)
        mats[c, 0, 64:128, :] = jnp.concatenate([block(1, 5), block(1, 0)], axis=1)
        zero = jnp.zeros((64, 64), BF16)
        for k, m in enumerate(slots(sx, sy)):
            mats[c, k + 1, 0:64, :] = jnp.concatenate([block(0, m), zero], axis=1)
            mats[c, k + 1, 64:128, :] = jnp.concatenate([zero, block(1, m)], axis=1)

    def told(d, x, y, z, fact):
        return jnp.where(inside[d], facts_in[DIRECTIONS.index(d), place(x, y, z, fact)], NOWHERE)

    def combine(source, target, names, flipped, origin, targets):
        def lane_ids(pair):
            first, second = (((mx + origin[0] + t[0]) * ny + my + origin[1] + t[1]) for t in pair)
            return jnp.where(even_row, second, first) if flipped else jnp.where(even_row, first, second)

        ids = [lane_ids(pair) for pair in names]
        for z in range(2):
            rows = slice(64 * z, 64 * z + 64)
            boxes = targets(z)
            total = [None, None, None]
            for j in (1, 0, 2):
                straight = source[j, rows, :].astype(F32)
                turned = pltpu.roll(straight, 64, 1)
                for value, lanes in (
                    (straight, jnp.where(left, boxes[2 * j], boxes[2 * j + 1])),
                    (turned, jnp.where(left, boxes[2 * j + 1], boxes[2 * j])),
                ):
                    for t in range(3):
                        if t == 2 and j != 1:
                            continue
                        term = value * (lanes == ids[t]).astype(F32)
                        total[t] = term if total[t] is None else total[t] + term
            for t in range(3):
                target[t, rows, :] = total[t].astype(BF16)

    for d in DIRECTIONS:
        when(d, facts_copies[d].wait_recv)
    for c, (sx, sy) in enumerate(CORNERS):
        x, y = (sx + 1) // 2, (sy + 1) // 2
        combine(
            raw.at[c], tiles.at[c], element_tiles(sx, sy), False, (0, 0),
            lambda z: [facts[place(x, y, z, fact)] for fact in range(4)]
            + [told((sx, 0), 1 - x, y, z, 4), told((0, sy), x, 1 - y, z, 5)],
        )

    for c, (sx, sy) in enumerate(CORNERS):
        blocks = {}
        for t, pair in enumerate(element_tiles(sx, sy)):
            turned = tiles[c, t].astype(F32).T
            blocks[pair[0]] = jnp.where(top, turned[0:64], turned[64:128]).astype(BF16)
            blocks[pair[1]] = jnp.where(top, turned[64:128], turned[0:64]).astype(BF16)
        ptd[c] = blocks[sx, sy]
        for r, offset in enumerate(FACES + ((0, 0),)):
            ptg[64 * r : 64 * r + 64, 128 * c : 128 * c + 128] = blocks[offset]

    def product(mat, ref, c):
        rows = dot(mat, jnp.concatenate([ref[c, 0], ref[c, 1], ref[c, 2]], axis=1))
        return rows[:, 0:128], rows[:, 128:256], rows[:, 256:384]

    nothing = jnp.zeros((128, 128), F32)
    for c, (sx, sy) in enumerate(CORNERS):
        s0, s1, s2 = product(mats[c, 0], tiles, c)
        x0, x1, x2 = product(mats[c, 1], tiles, corner(-sx, sy))
        y0, y1, y2 = product(mats[c, 2], tiles, corner(sx, -sy))
        im[c, 0] = s0 + jnp.where(even, x0 + y0, nothing)
        im[c, 1] = s1 + jnp.where(even, x2 + y1, x1 + y2)
        im[c, 2] = s2 + jnp.where(even, x1 + y2, x2 + y1)
        im[c, 3] = jnp.where(even, nothing, y0)
        im[c, 4] = jnp.where(even, nothing, x0)

    for jx in range(7):
        for jy in range(7):
            if abs(jx - 3) + abs(jy - 3) > 3:
                out[0, 0, jx, jy] = jnp.zeros((64, 64), BF16)

    first_copies, rest_copies, face_copies = {}, {}, {}
    for c, (sx, sy) in enumerate(CORNERS):
        x, y = (sx + 1) // 2, (sy + 1) // 2
        when((sx, 0), copies_x[c].wait_recv)
        combine(
            raw_x.at[c], tiles_x.at[c], element_tiles(-sx, sy), False, (sx, 0),
            lambda z: [told((sx, 0), 1 - x, y, z, fact) for fact in range(4)]
            + [facts[place(x, y, z, 4)], told((sx, sy), 1 - x, 1 - y, z, 5)],
        )
        x0, x1, x2 = product(mats[c, 3], tiles_x, c)
        im[c, 0] += x1
        im[c, 1] += x0
        im[c, 3] += x2
        first = jnp.concatenate([im[c, 2].astype(BF16), im[c, 3].astype(BF16)], axis=1)
        first_out[c] = dot(ptd[c], first).astype(BF16)
        to = corner(-sx, -sy)
        first_copies[to] = remote(first_out.at[c], first_in.at[to], (first_s, first_r), to, (sx, sy))
        when((sx, sy), first_copies[to].start)

    for c, (sx, sy) in enumerate(CORNERS):
        x, y = (sx + 1) // 2, (sy + 1) // 2
        when((0, sy), copies_y[c].wait_recv)
        combine(
            raw_y.at[c], tiles_y.at[c], element_tiles(sx, -sy), True, (0, sy),
            lambda z: [told((0, sy), x, 1 - y, z, fact) for fact in range(4)]
            + [told((sx, sy), 1 - x, 1 - y, z, 4), facts[place(x, y, z, 5)]],
        )
        y0, y1, y2 = product(mats[c, 4], tiles_y, c)
        image = [
            (im[c, 0] + y1).astype(BF16), (im[c, 1] + y0).astype(BF16), im[c, 2].astype(BF16),
            im[c, 3].astype(BF16), (im[c, 4] + y2).astype(BF16),
        ]
        rest_out[c] = dot(ptd[c], jnp.concatenate([image[0], image[1], image[4]], axis=1)).astype(BF16)
        to = corner(-sx, -sy)
        rest_copies[to] = remote(rest_out.at[c], rest_in.at[to], (rest_s, rest_r), to, (sx, sy))
        when((sx, sy), rest_copies[to].start)
        names = image_tiles(sx, sy)
        at_even = {pair[0]: i for i, pair in enumerate(names)}
        at_odd = {pair[1]: i for i, pair in enumerate(names)}
        for g, (e, o) in enumerate(PAIRS):
            evens = image[at_even[e]].astype(F32) if e in at_even else nothing
            odds = image[at_odd[o]].astype(F32) if o in at_odd else nothing
            imw[128 * c : 128 * c + 128, 128 * g : 128 * g + 128] = jnp.where(even, evens, odds).astype(BF16)

    wide = imw[...]
    for first in (2, 0):
        rows = dot(ptg[64 * first : 64 * first + 128, :], wide).astype(BF16)
        for k in (first, first + 1):
            dx, dy = FACES[k]
            to = FACES.index((-dx, -dy))
            face_out[k] = rows[64 * (k - first) : 64 * (k - first) + 64]
            face_copies[to] = remote(face_out.at[k], face_in.at[to], (face_s, face_r), to, (dx, dy))
            when((dx, dy), face_copies[to].start)

    offsets = [(dx, dy) for dx in range(-3, 4) for dy in range(-3, 4) if abs(dx) + abs(dy) <= 3]
    at = {offset: i for i, offset in enumerate(offsets)}
    own = dot(ptg[256:320, :], wide)
    for offset in offsets:
        acc[at[offset]] = jnp.zeros((64, 128), F32)
    for g, pair in enumerate(PAIRS):
        for offset in pair:
            if offset is not None:
                acc[at[offset]] = own[:, 128 * g : 128 * g + 128]

    def gather(d, copy, ref, names):
        def action():
            copy.wait_recv()
            for g, pair in enumerate(names):
                tile = ref[:, 128 * g : 128 * g + 128].astype(F32)
                for offset in pair:
                    if offset is not None:
                        acc[at[add(offset, d)]] += tile

        when(d, action)

    for c, (sx, sy) in enumerate(CORNERS):
        gather((sx, sy), first_copies[c], first_in.at[c], image_tiles(-sx, -sy)[2:4])
    for k in (0, 1):
        gather(FACES[k], face_copies[k], face_in.at[k], PAIRS)
    for c, (sx, sy) in enumerate(CORNERS):
        names = image_tiles(-sx, -sy)
        gather((sx, sy), rest_copies[c], rest_in.at[c], (names[0], names[1], names[4]))
    for k in (2, 3):
        gather(FACES[k], face_copies[k], face_in.at[k], PAIRS)

    for offset in offsets:
        value = acc[at[offset]]
        other = pltpu.roll(value, 64, 1)
        straight = top if offset[1] % 2 == 0 else jnp.logical_not(top)
        out[0, 0, offset[0] + 3, offset[1] + 3] = jnp.where(straight, value, other)[:, 0:64].astype(BF16)

    for dx, dy in DIRECTIONS:
        when((-dx, -dy), facts_copies[dx, dy].wait_send)
    for k, (dx, dy) in enumerate(FACES):
        when((-dx, -dy), face_copies[k].wait_send)
    for c, (sx, sy) in enumerate(CORNERS):
        when((-sx, 0), copies_x[c].wait_send)
        when((0, -sy), copies_y[c].wait_send)
        when((-sx, -sy), first_copies[c].wait_send)
        when((-sx, -sy), rest_copies[c].wait_send)


def per_device(fine_matrix, prolongator, aggregate, face_links):
    nx, ny = lax.axis_size("sx"), lax.axis_size("sy")
    dma = pltpu.SemaphoreType.DMA
    return pl.pallas_call(
        functools.partial(kernel, nx, ny),
        out_shape=jax.ShapeDtypeStruct((1, 1, 7, 7, 64, 64), BF16),
        in_specs=[pl.BlockSpec(memory_space=pl.ANY)] * 4,
        out_specs=pl.BlockSpec(memory_space=pltpu.VMEM),
        scratch_shapes=[
            pltpu.VMEM((2, 2, 2, 7, 64, 64), BF16),
            pltpu.VMEM((2, 2, 2, 7, 64, 64), BF16),
            pltpu.SMEM((2, 2, 2), jnp.int32),
            pltpu.SMEM((2, 2, 2, 6), jnp.int32),
            pltpu.SMEM((64,), jnp.int32),
            pltpu.SMEM((8, 64), jnp.int32),
            *[pltpu.VMEM((4, 3, 128, 128), BF16)] * 6,
            pltpu.VMEM((4, 5, 128, 128), BF16),
            pltpu.VMEM((4, 5, 128, 128), F32),
            pltpu.VMEM((320, 512), BF16),
            pltpu.VMEM((4, 64, 128), BF16),
            pltpu.VMEM((512, 896), BF16),
            *[pltpu.VMEM((4, 64, 896), BF16)] * 2,
            *[pltpu.VMEM((4, 64, 256), BF16)] * 2,
            *[pltpu.VMEM((4, 64, 384), BF16)] * 2,
            pltpu.VMEM((25, 64, 128), F32),
            dma((2,)),
            dma((4,)),
            dma((4,)),
            *[dma((8,))] * 4,
            *[dma((4,))] * 6,
        ],
        compiler_params=pltpu.CompilerParams(
            collective_id=0, has_side_effects=True, vmem_limit_bytes=60 * 1024 * 1024
        ),
        name="galerkin",
    )(fine_matrix, prolongator, aggregate, face_links)


def solution(mesh):
    return jax.shard_map(
        per_device,
        mesh=mesh,
        in_specs=(
            P("sx", "sy", None, None, None, None),
            P("sx", "sy", None, None, None, None),
            P("sx", "sy", None),
            P("sx", "sy", None, None),
        ),
        out_specs=P("sx", "sy", None, None, None, None),
        check_vma=False,
    )
```

time: 31.1 us -> 22.9 us (0.74)
  the two profiles are of different devices: /device:TPU:0 before, /device:TPU:39 now
where the time goes in v2:
time: 22.9 us; the launch traced here: 22.7 us
  Pallas kernels  20.7 us (90%)
  local copies, waits for them, and re-layouts  2.08 us (9%)
    pallas_call x1, Pallas kernels, per_device(): pl.pallas_call(functools.partial(kernel, nx, ny), out_shape=jax.ShapeDtyp...  20.7 us
    unnamed x1, local copies, waits for them, and re-layouts  2.08 us

profile of v2, /device:TPU:39, one launch (start us, length us, event | category | flops | bytes accessed | tf_op | source)
XLA Modules:
  0.0 22.7 jit_solution(2515005677472399744)
XLA Ops:
  0.0 20.7 %galerkin.1 = bf16[1,1,7,7,64,64]{5,4,3,2,1,0:T(8,128)(2,1)} custom-call(bf16[2,2,2,7,64,64]{5,4,3,2,1,0:T(8,128)(2,1)} %a_hbm.1, bf16[2,2,2,7,64,64]{5,4,3,2,1,0:T(8,128)(2,1)} %p_hbm.1, s32[2,2,2]{2,1,0:T(2,128)} %agg_hbm.1, s32[2,2,2,6]{3,2,1,0:T(2,128)} %links_hbm.1), custom_call_target="tpu_custom_call" | custom-call | tf_op jit(solution)/shard_map/galerkin/pallas_call | solution.py:334
  20.7 2.1 %copy.6 = bf16[1,1,7,7,64,64]{5,4,3,2,1,0:T(8,128)(2,1)} copy(bf16[1,1,7,7,64,64]{5,4,3,2,1,0:T(8,128)(2,1)} %galerkin.1) | data formatting | bytes 802816

commit v3 on v2

--- a/solution.py
+++ b/solution.py
@@ -360,10 +360,10 @@
             *[dma((4,))] * 6,
         ],
         compiler_params=pltpu.CompilerParams(
-            collective_id=0, has_side_effects=True, vmem_limit_bytes=60 * 1024 * 1024
+            collective_id=0, has_side_effects=True, vmem_limit_bytes=32 * 1024 * 1024
         ),
         name="galerkin",
-    )(fine_matrix, prolongator, aggregate, face_links)
+    )(*(pltpu.with_memory_space_constraint(v, pltpu.HBM) for v in (fine_matrix, prolongator, aggregate, face_links)))
 
 
 def solution(mesh):

time: 22.9 us -> 20.8 us (0.908)
  local copies, waits for them, and re-layouts: 2.08 us -> 0.89 us
  Pallas kernels: 20.7 us -> 19.8 us
    unnamed x1, local copies, waits for them, and re-layouts: 2.08 us -> 0.89 us
    pallas_call x1, Pallas kernels: 20.7 us -> 19.8 us  [per_device(): pl.pallas_call(functools.partial(kernel, nx, ny), out_shape=jax.ShapeDtyp...]
where the time goes in v3:
time: 20.8 us; the launch traced here: 20.7 us
  Pallas kernels  19.8 us (95%)
  local copies, waits for them, and re-layouts  0.89 us (4%)
    pallas_call x1, Pallas kernels, per_device(): pl.pallas_call(functools.partial(kernel, nx, ny), out_shape=jax.ShapeDtyp...  19.8 us
    unnamed x1, local copies, waits for them, and re-layouts  0.89 us

profile of v3, /device:TPU:39, one launch (start us, length us, event | category | flops | bytes accessed | tf_op | source)
XLA Modules:
  0.0 20.7 jit_solution(10889846840637322800)
XLA Ops:
  0.0 19.8 %galerkin.1 = bf16[1,1,7,7,64,64]{5,4,3,2,1,0:T(8,128)(2,1)S(1)} custom-call(bf16[2,2,2,7,64,64]{5,4,3,2,1,0:T(8,128)(2,1)} %a_hbm.1, bf16[2,2,2,7,64,64]{5,4,3,2,1,0:T(8,128)(2,1)} %p_hbm.1, s32[2,2,2]{2,1,0:T(2,128)} %agg_hbm.1, s32[2,2,2,6]{3,2,1,0:T(2,128)} %links_hbm.1), custom_call_target="tpu_custom_call" | custom-call | tf_op jit(solution)/shard_map/galerkin/pallas_call | solution.py:334
  19.8 0.9 %copy.6 = bf16[1,1,7,7,64,64]{5,4,3,2,1,0:T(8,128)(2,1)} copy(bf16[1,1,7,7,64,64]{5,4,3,2,1,0:T(8,128)(2,1)S(1)} %galerkin.1) | data formatting | bytes 802816

commit v4 on v3

--- a/solution.py
+++ b/solution.py
@@ -62,8 +62,20 @@
     for sx, sy in CORNERS:
         inside[sx, sy] = jnp.logical_and(inside[sx, 0], inside[0, sy])
 
-    def when(d, action):
-        pl.when(inside[d])(action)
+    interior = jnp.logical_and(
+        jnp.logical_and(inside[-1, 0], inside[1, 0]), jnp.logical_and(inside[0, -1], inside[0, 1])
+    )
+
+    def each(actions):
+        @pl.when(interior)
+        def _():
+            for _, action in actions:
+                action()
+
+        @pl.when(jnp.logical_not(interior))
+        def _():
+            for d, action in actions:
+                pl.when(inside[d])(action)
 
     def remote(src, dst, sems, k, d):
         return pltpu.make_async_remote_copy(
@@ -72,8 +84,10 @@
         )
 
     barrier = pltpu.get_barrier_semaphore()
-    for d in DIRECTIONS:
-        when(d, lambda: pl.semaphore_signal(barrier, inc=1, device_id=device(*d), device_id_type=MESH))
+    def greet(d):
+        return d, lambda: pl.semaphore_signal(barrier, inc=1, device_id=device(*d), device_id_type=MESH)
+
+    each([greet(d) for d in DIRECTIONS])
     scalar_loads = (
         pltpu.make_async_copy(agg_hbm, agg, scalar_sem.at[0]),
         pltpu.make_async_copy(links_hbm, links, scalar_sem.at[1]),
@@ -86,20 +100,26 @@
     for copy in (*scalar_loads, *p_loads, *a_loads):
         copy.start()
 
-    left = lax.broadcasted_iota(jnp.int32, (1, 128), 1) < 64
     even_row = (lax.broadcasted_iota(jnp.int32, (1, 128), 1) >= 64).astype(jnp.int32) == par
     even = (lax.broadcasted_iota(jnp.int32, (128, 128), 1) >= 64).astype(jnp.int32) == par
     top = jnp.full((64, 128), par, jnp.int32) == 0
 
-    for side in FACES:
-
-        @pl.when(jnp.logical_not(inside[side]))
-        def _():
-            for c, (sx, sy) in enumerate(CORNERS):
-                if side == (sx, 0):
-                    raw_x[c] = jnp.zeros((3, 128, 128), BF16)
-                if side == (0, sy):
-                    raw_y[c] = jnp.zeros((3, 128, 128), BF16)
+    @pl.when(jnp.logical_not(interior))
+    def _():
+        for k, d in enumerate(DIRECTIONS):
+
+            @pl.when(jnp.logical_not(inside[d]))
+            def _():
+                if k < 4:
+                    face_in[k] = jnp.zeros((64, 896), BF16)
+                else:
+                    first_in[k - 4] = jnp.zeros((64, 256), BF16)
+                    rest_in[k - 4] = jnp.zeros((64, 384), BF16)
+                for c, (sx, sy) in enumerate(CORNERS):
+                    if d == (sx, 0):
+                        raw_x[c] = jnp.zeros((3, 128, 128), BF16)
+                    if d == (0, sy):
+                        raw_y[c] = jnp.zeros((3, 128, 128), BF16)
 
     def place(x, y, z, fact):
         return FACTS * (4 * x + 2 * y + z) + fact
@@ -118,28 +138,33 @@
             ):
                 facts[place(x, y, z, fact)] = jnp.where(links[x, y, z, m - 1] == 1, target, NOWHERE)
 
-    for c, (sx, sy) in enumerate(CORNERS):
-        x, y = (sx + 1) // 2, (sy + 1) // 2
-        ix, iy, ox, oy = slots(sx, sy)
-        p_loads[c].wait()
-        for z in range(2):
-            for j, (m, n) in enumerate(((0, 6 if z == 0 else 5), (ix, iy), (ox, oy))):
-                raw[c, j, 64 * z : 64 * z + 64, :] = jnp.concatenate([p_v[x, y, z, m], p_v[x, y, z, n]], axis=1)
+    def pack(evens_first):
+        for c, (sx, sy) in enumerate(CORNERS):
+            x, y = (sx + 1) // 2, (sy + 1) // 2
+            ix, iy, ox, oy = slots(sx, sy)
+            p_loads[c].wait()
+            for z in range(2):
+                for j, (m, n) in enumerate(((0, 6 if z == 0 else 5), (ix, iy), (ox, oy))):
+                    pair = [p_v[x, y, z, m], p_v[x, y, z, n]]
+                    raw[c, j, 64 * z : 64 * z + 64, :] = jnp.concatenate(pair if evens_first else pair[::-1], axis=1)
+
+    pl.when(par == 0)(lambda: pack(True))
+    pl.when(par == 1)(lambda: pack(False))
 
     pl.semaphore_wait(barrier, sum(there.astype(jnp.int32) for there in inside.values()))
 
     facts_copies = {}
     for k, (dx, dy) in enumerate(DIRECTIONS):
         facts_copies[dx, dy] = remote(facts, facts_in.at[k], (facts_s, facts_r), k, (-dx, -dy))
-        when((-dx, -dy), facts_copies[dx, dy].start)
     copies_x, copies_y = [], []
     for c, (sx, sy) in enumerate(CORNERS):
         copies_x.append(remote(raw.at[corner(-sx, sy)], raw_x.at[c], (raw_s, raw_r), c, (-sx, 0)))
         copies_y.append(remote(raw.at[corner(sx, -sy)], raw_y.at[c], (raw_s, raw_r), 4 + c, (0, -sy)))
-    for c, (sx, sy) in enumerate(CORNERS):
-        when((0, -sy), copies_y[c].start)
-    for c, (sx, sy) in enumerate(CORNERS):
-        when((-sx, 0), copies_x[c].start)
+    each(
+        [((-dx, -dy), facts_copies[dx, dy].start) for dx, dy in CORNERS + FACES]
+        + [((0, -sy), copies_y[c].start) for c, (sx, sy) in enumerate(CORNERS)]
+        + [((-sx, 0), copies_x[c].start) for c, (sx, sy) in enumerate(CORNERS)]
+    )
 
     for c, (sx, sy) in enumerate(CORNERS):
         x, y = (sx + 1) // 2, (sy + 1) // 2
@@ -167,27 +192,24 @@
             return jnp.where(even_row, second, first) if flipped else jnp.where(even_row, first, second)
 
         ids = [lane_ids(pair) for pair in names]
+        swapped = [lane_ids(pair[::-1]) for pair in names]
+        evens = jnp.logical_not(even_row) if flipped else even_row
         for z in range(2):
             rows = slice(64 * z, 64 * z + 64)
             boxes = targets(z)
-            total = [None, None, None]
-            for j in (1, 0, 2):
-                straight = source[j, rows, :].astype(F32)
-                turned = pltpu.roll(straight, 64, 1)
-                for value, lanes in (
-                    (straight, jnp.where(left, boxes[2 * j], boxes[2 * j + 1])),
-                    (turned, jnp.where(left, boxes[2 * j + 1], boxes[2 * j])),
-                ):
-                    for t in range(3):
-                        if t == 2 and j != 1:
-                            continue
-                        term = value * (lanes == ids[t]).astype(F32)
-                        total[t] = term if total[t] is None else total[t] + term
-            for t in range(3):
-                target[t, rows, :] = total[t].astype(BF16)
-
-    for d in DIRECTIONS:
-        when(d, facts_copies[d].wait_recv)
+            values = [source[j, rows, :].astype(F32) for j in range(3)]
+            lanes = [jnp.where(evens, boxes[2 * j], boxes[2 * j + 1]) for j in range(3)]
+
+            def picked(names, which):
+                return sum(values[j] * (lanes[j] == names).astype(F32) for j in which)
+
+            target[0, rows, :] = (
+                picked(ids[0], (0, 1, 2)) + pltpu.roll(picked(swapped[0], (0, 1, 2)), 64, 1)
+            ).astype(BF16)
+            target[1, rows, :] = (picked(ids[1], (0, 2)) + pltpu.roll(picked(swapped[1], (0, 1)), 64, 1)).astype(BF16)
+            target[2, rows, :] = picked(ids[2], (1,)).astype(BF16)
+
+    each([(d, facts_copies[d].wait_recv) for d in DIRECTIONS])
     for c, (sx, sy) in enumerate(CORNERS):
         x, y = (sx + 1) // 2, (sy + 1) // 2
         combine(
@@ -226,106 +248,139 @@
             if abs(jx - 3) + abs(jy - 3) > 3:
                 out[0, 0, jx, jy] = jnp.zeros((64, 64), BF16)
 
-    first_copies, rest_copies, face_copies = {}, {}, {}
+    each([((sx, 0), copies_x[c].wait_recv) for c, (sx, sy) in enumerate(CORNERS)])
     for c, (sx, sy) in enumerate(CORNERS):
         x, y = (sx + 1) // 2, (sy + 1) // 2
-        when((sx, 0), copies_x[c].wait_recv)
         combine(
             raw_x.at[c], tiles_x.at[c], element_tiles(-sx, sy), False, (sx, 0),
             lambda z: [told((sx, 0), 1 - x, y, z, fact) for fact in range(4)]
             + [facts[place(x, y, z, 4)], told((sx, sy), 1 - x, 1 - y, z, 5)],
         )
+    for c in range(4):
         x0, x1, x2 = product(mats[c, 3], tiles_x, c)
         im[c, 0] += x1
         im[c, 1] += x0
         im[c, 3] += x2
+    for c in range(4):
         first = jnp.concatenate([im[c, 2].astype(BF16), im[c, 3].astype(BF16)], axis=1)
         first_out[c] = dot(ptd[c], first).astype(BF16)
-        to = corner(-sx, -sy)
-        first_copies[to] = remote(first_out.at[c], first_in.at[to], (first_s, first_r), to, (sx, sy))
-        when((sx, sy), first_copies[to].start)
-
-    for c, (sx, sy) in enumerate(CORNERS):
-        x, y = (sx + 1) // 2, (sy + 1) // 2
-        when((0, sy), copies_y[c].wait_recv)
-        combine(
-            raw_y.at[c], tiles_y.at[c], element_tiles(sx, -sy), True, (0, sy),
-            lambda z: [told((0, sy), x, 1 - y, z, fact) for fact in range(4)]
-            + [told((sx, sy), 1 - x, 1 - y, z, 4), facts[place(x, y, z, 5)]],
-        )
-        y0, y1, y2 = product(mats[c, 4], tiles_y, c)
-        image = [
-            (im[c, 0] + y1).astype(BF16), (im[c, 1] + y0).astype(BF16), im[c, 2].astype(BF16),
-            im[c, 3].astype(BF16), (im[c, 4] + y2).astype(BF16),
-        ]
-        rest_out[c] = dot(ptd[c], jnp.concatenate([image[0], image[1], image[4]], axis=1)).astype(BF16)
-        to = corner(-sx, -sy)
-        rest_copies[to] = remote(rest_out.at[c], rest_in.at[to], (rest_s, rest_r), to, (sx, sy))
-        when((sx, sy), rest_copies[to].start)
-        names = image_tiles(sx, sy)
-        at_even = {pair[0]: i for i, pair in enumerate(names)}
-        at_odd = {pair[1]: i for i, pair in enumerate(names)}
-        for g, (e, o) in enumerate(PAIRS):
-            evens = image[at_even[e]].astype(F32) if e in at_even else nothing
-            odds = image[at_odd[o]].astype(F32) if o in at_odd else nothing
-            imw[128 * c : 128 * c + 128, 128 * g : 128 * g + 128] = jnp.where(even, evens, odds).astype(BF16)
+    first_copies = [
+        remote(first_out.at[corner(-sx, -sy)], first_in.at[c], (first_s, first_r), c, (-sx, -sy))
+        for c, (sx, sy) in enumerate(CORNERS)
+    ]
+    each([((-sx, -sy), first_copies[c].start) for c, (sx, sy) in enumerate(CORNERS)])
+
+    rest_copies = [
+        remote(rest_out.at[corner(-sx, -sy)], rest_in.at[c], (rest_s, rest_r), c, (-sx, -sy))
+        for c, (sx, sy) in enumerate(CORNERS)
+    ]
+    for group in ((0, 1), (2, 3)):
+        each([((0, CORNERS[c][1]), copies_y[c].wait_recv) for c in group])
+        for c in group:
+            sx, sy = CORNERS[c]
+            x, y = (sx + 1) // 2, (sy + 1) // 2
+            combine(
+                raw_y.at[c], tiles_y.at[c], element_tiles(sx, -sy), True, (0, sy),
+                lambda z: [told((0, sy), x, 1 - y, z, fact) for fact in range(4)]
+                + [told((sx, sy), 1 - x, 1 - y, z, 4), facts[place(x, y, z, 5)]],
+            )
+        for c in group:
+            sx, sy = CORNERS[c]
+            y0, y1, y2 = product(mats[c, 4], tiles_y, c)
+            image = [im[c, 0] + y1, im[c, 1] + y0, im[c, 2], im[c, 3], im[c, 4] + y2]
+            rest = jnp.concatenate([image[0].astype(BF16), image[1].astype(BF16), image[4].astype(BF16)], axis=1)
+            rest_out[c] = dot(ptd[c], rest).astype(BF16)
+            names = image_tiles(sx, sy)
+            at_even = {pair[0]: i for i, pair in enumerate(names)}
+            at_odd = {pair[1]: i for i, pair in enumerate(names)}
+            for g, (e, o) in enumerate(PAIRS):
+                evens = image[at_even[e]] if e in at_even else nothing
+                odds = image[at_odd[o]] if o in at_odd else nothing
+                imw[128 * c : 128 * c + 128, 128 * g : 128 * g + 128] = jnp.where(even, evens, odds).astype(BF16)
+        each([(CORNERS[c], rest_copies[3 - c].start) for c in group])
 
     wide = imw[...]
+    face_copies = [
+        remote(face_out.at[FACES.index((-dx, -dy))], face_in.at[k], (face_s, face_r), k, (-dx, -dy))
+        for k, (dx, dy) in enumerate(FACES)
+    ]
     for first in (2, 0):
         rows = dot(ptg[64 * first : 64 * first + 128, :], wide).astype(BF16)
-        for k in (first, first + 1):
-            dx, dy = FACES[k]
-            to = FACES.index((-dx, -dy))
-            face_out[k] = rows[64 * (k - first) : 64 * (k - first) + 64]
-            face_copies[to] = remote(face_out.at[k], face_in.at[to], (face_s, face_r), to, (dx, dy))
-            when((dx, dy), face_copies[to].start)
+        face_out[first] = rows[0:64]
+        face_out[first + 1] = rows[64:128]
+        each([((-FACES[k][0], -FACES[k][1]), face_copies[k].start) for k in (first, first + 1)])
 
     offsets = [(dx, dy) for dx in range(-3, 4) for dy in range(-3, 4) if abs(dx) + abs(dy) <= 3]
     at = {offset: i for i, offset in enumerate(offsets)}
+
+    def tiles_of(ref, names, d):
+        return [
+            (add(offset, d), ref, g) for g, pair in enumerate(names) for offset in pair if offset is not None
+        ]
+
     own = dot(ptg[256:320, :], wide)
+    mine = {offset: g for g, pair in enumerate(PAIRS) for offset in pair if offset is not None}
+    early = [source for k in (0, 1) for source in tiles_of(face_in.at[k], PAIRS, FACES[k])]
+    late = []
+    for c, (sx, sy) in enumerate(CORNERS):
+        names = image_tiles(-sx, -sy)
+        early.extend(tiles_of(first_in.at[c], names[2:4], (sx, sy)))
+        late.extend(tiles_of(rest_in.at[c], (names[0], names[1], names[4]), (sx, sy)))
+
+    def gathered(total, offset, sources):
+        for name, ref, g in sources:
+            if name == offset:
+                tile = ref[:, 128 * g : 128 * g + 128].astype(F32)
+                total = tile if total is None else total + tile
+        return jnp.zeros((64, 128), F32) if total is None else total
+
+    each(
+        [((sx, sy), first_copies[c].wait_recv) for c, (sx, sy) in enumerate(CORNERS)]
+        + [(FACES[k], face_copies[k].wait_recv) for k in (0, 1)]
+    )
     for offset in offsets:
-        acc[at[offset]] = jnp.zeros((64, 128), F32)
-    for g, pair in enumerate(PAIRS):
-        for offset in pair:
-            if offset is not None:
-                acc[at[offset]] = own[:, 128 * g : 128 * g + 128]
-
-    def gather(d, copy, ref, names):
-        def action():
-            copy.wait_recv()
-            for g, pair in enumerate(names):
-                tile = ref[:, 128 * g : 128 * g + 128].astype(F32)
+        g = mine.get(offset)
+        acc[at[offset]] = gathered(None if g is None else own[:, 128 * g : 128 * g + 128], offset, early)
+    each([((sx, sy), rest_copies[c].wait_recv) for c, (sx, sy) in enumerate(CORNERS)])
+
+    def finish(evens_first):
+        def on_left(value, offset):
+            return value if (offset[1] % 2 == 0) == evens_first else pltpu.roll(value, 64, 1)
+
+        def put(offset, value):
+            out[0, 0, offset[0] + 3, offset[1] + 3] = value[:, 0:64].astype(BF16)
+
+        last = {}
+        for k in (2, 3):
+            for g, pair in enumerate(PAIRS):
                 for offset in pair:
                     if offset is not None:
-                        acc[at[add(offset, d)]] += tile
-
-        when(d, action)
-
-    for c, (sx, sy) in enumerate(CORNERS):
-        gather((sx, sy), first_copies[c], first_in.at[c], image_tiles(-sx, -sy)[2:4])
-    for k in (0, 1):
-        gather(FACES[k], face_copies[k], face_in.at[k], PAIRS)
-    for c, (sx, sy) in enumerate(CORNERS):
-        names = image_tiles(-sx, -sy)
-        gather((sx, sy), rest_copies[c], rest_in.at[c], (names[0], names[1], names[4]))
-    for k in (2, 3):
-        gather(FACES[k], face_copies[k], face_in.at[k], PAIRS)
-
-    for offset in offsets:
-        value = acc[at[offset]]
-        other = pltpu.roll(value, 64, 1)
-        straight = top if offset[1] % 2 == 0 else jnp.logical_not(top)
-        out[0, 0, offset[0] + 3, offset[1] + 3] = jnp.where(straight, value, other)[:, 0:64].astype(BF16)
-
-    for dx, dy in DIRECTIONS:
-        when((-dx, -dy), facts_copies[dx, dy].wait_send)
-    for k, (dx, dy) in enumerate(FACES):
-        when((-dx, -dy), face_copies[k].wait_send)
-    for c, (sx, sy) in enumerate(CORNERS):
-        when((-sx, 0), copies_x[c].wait_send)
-        when((0, -sy), copies_y[c].wait_send)
-        when((-sx, -sy), first_copies[c].wait_send)
-        when((-sx, -sy), rest_copies[c].wait_send)
+                        last.setdefault(add(offset, FACES[k]), []).append((k, g))
+        for offset in offsets:
+            value = on_left(gathered(acc[at[offset]], offset, late), offset)
+            if offset in last:
+                acc[at[offset]] = value
+            else:
+                put(offset, value)
+        each([(FACES[k], face_copies[k].wait_recv) for k in (2, 3)])
+        for offset in offsets:
+            if offset in last:
+                value = acc[at[offset]]
+                for k, g in last[offset]:
+                    value += on_left(face_in[k, :, 128 * g : 128 * g + 128].astype(F32), offset)
+                put(offset, value)
+
+    pl.when(par == 0)(lambda: finish(True))
+    pl.when(par == 1)(lambda: finish(False))
+
+    each(
+        [((-dx, -dy), facts_copies[dx, dy].wait_send) for dx, dy in DIRECTIONS]
+        + [((-dx, -dy), face_copies[k].wait_send) for k, (dx, dy) in enumerate(FACES)]
+        + [((-sx, 0), copies_x[c].wait_send) for c, (sx, sy) in enumerate(CORNERS)]
+        + [((0, -sy), copies_y[c].wait_send) for c, (sx, sy) in enumerate(CORNERS)]
+        + [((-sx, -sy), first_copies[c].wait_send) for c, (sx, sy) in enumerate(CORNERS)]
+        + [((-sx, -sy), rest_copies[c].wait_send) for c, (sx, sy) in enumerate(CORNERS)]
+    )
 
 
 def per_device(fine_matrix, prolongator, aggregate, face_links):

time: 20.8 us -> 20.2 us (0.971)
  Pallas kernels: 19.8 us -> 19.2 us
    pallas_call x1, Pallas kernels: 19.8 us -> 19.2 us  [per_device(): pl.pallas_call(functools.partial(kernel, nx, ny), out_shape=jax.ShapeDtyp...]
where the time goes in v4:
time: 20.2 us; the launch traced here: 20.1 us
  Pallas kernels  19.2 us (95%)
  local copies, waits for them, and re-layouts  0.89 us (4%)
    pallas_call x1, Pallas kernels, per_device(): pl.pallas_call(functools.partial(kernel, nx, ny), out_shape=jax.ShapeDtyp...  19.2 us
    unnamed x1, local copies, waits for them, and re-layouts  0.89 us

profile of v4, /device:TPU:39, one launch (start us, length us, event | category | flops | bytes accessed | tf_op | source)
XLA Modules:
  0.0 20.1 jit_solution(15435326623080641012)
XLA Ops:
  0.0 19.2 %galerkin.1 = bf16[1,1,7,7,64,64]{5,4,3,2,1,0:T(8,128)(2,1)S(1)} custom-call(bf16[2,2,2,7,64,64]{5,4,3,2,1,0:T(8,128)(2,1)} %a_hbm.1, bf16[2,2,2,7,64,64]{5,4,3,2,1,0:T(8,128)(2,1)} %p_hbm.1, s32[2,2,2]{2,1,0:T(2,128)} %agg_hbm.1, s32[2,2,2,6]{3,2,1,0:T(2,128)} %links_hbm.1), custom_call_target="tpu_custom_call" | custom-call | tf_op jit(solution)/shard_map/galerkin/pallas_call | solution.py:389
  19.2 0.9 %copy.6 = bf16[1,1,7,7,64,64]{5,4,3,2,1,0:T(8,128)(2,1)} copy(bf16[1,1,7,7,64,64]{5,4,3,2,1,0:T(8,128)(2,1)S(1)} %galerkin.1) | data formatting | bytes 802816

commit v5 on v4

--- a/solution.py
+++ b/solution.py
@@ -113,11 +113,11 @@
                 if k < 4:
                     face_in[k] = jnp.zeros((64, 896), BF16)
                 else:
-                    first_in[k - 4] = jnp.zeros((64, 256), BF16)
                     rest_in[k - 4] = jnp.zeros((64, 384), BF16)
                 for c, (sx, sy) in enumerate(CORNERS):
                     if d == (sx, 0):
                         raw_x[c] = jnp.zeros((3, 128, 128), BF16)
+                        first_in[c] = jnp.zeros((64, 256), BF16)
                     if d == (0, sy):
                         raw_y[c] = jnp.zeros((3, 128, 128), BF16)
 
@@ -209,7 +209,7 @@
             target[1, rows, :] = (picked(ids[1], (0, 2)) + pltpu.roll(picked(swapped[1], (0, 1)), 64, 1)).astype(BF16)
             target[2, rows, :] = picked(ids[2], (1,)).astype(BF16)
 
-    each([(d, facts_copies[d].wait_recv) for d in DIRECTIONS])
+    each([(d, facts_copies[d].wait_recv) for d in FACES])
     for c, (sx, sy) in enumerate(CORNERS):
         x, y = (sx + 1) // 2, (sy + 1) // 2
         combine(
@@ -248,7 +248,10 @@
             if abs(jx - 3) + abs(jy - 3) > 3:
                 out[0, 0, jx, jy] = jnp.zeros((64, 64), BF16)
 
-    each([((sx, 0), copies_x[c].wait_recv) for c, (sx, sy) in enumerate(CORNERS)])
+    each(
+        [(d, facts_copies[d].wait_recv) for d in CORNERS]
+        + [((sx, 0), copies_x[c].wait_recv) for c, (sx, sy) in enumerate(CORNERS)]
+    )
     for c, (sx, sy) in enumerate(CORNERS):
         x, y = (sx + 1) // 2, (sy + 1) // 2
         combine(
@@ -265,16 +268,16 @@
         first = jnp.concatenate([im[c, 2].astype(BF16), im[c, 3].astype(BF16)], axis=1)
         first_out[c] = dot(ptd[c], first).astype(BF16)
     first_copies = [
-        remote(first_out.at[corner(-sx, -sy)], first_in.at[c], (first_s, first_r), c, (-sx, -sy))
+        remote(first_out.at[corner(-sx, sy)], first_in.at[c], (first_s, first_r), c, (-sx, 0))
         for c, (sx, sy) in enumerate(CORNERS)
     ]
-    each([((-sx, -sy), first_copies[c].start) for c, (sx, sy) in enumerate(CORNERS)])
+    each([((-sx, 0), first_copies[c].start) for c, (sx, sy) in enumerate(CORNERS)])
 
     rest_copies = [
         remote(rest_out.at[corner(-sx, -sy)], rest_in.at[c], (rest_s, rest_r), c, (-sx, -sy))
         for c, (sx, sy) in enumerate(CORNERS)
     ]
-    for group in ((0, 1), (2, 3)):
+    for group in ((0,), (1,), (2,), (3,)):
         each([((0, CORNERS[c][1]), copies_y[c].wait_recv) for c in group])
         for c in group:
             sx, sy = CORNERS[c]
@@ -299,15 +302,36 @@
                 imw[128 * c : 128 * c + 128, 128 * g : 128 * g + 128] = jnp.where(even, evens, odds).astype(BF16)
         each([(CORNERS[c], rest_copies[3 - c].start) for c in group])
 
+    each([((sx, 0), first_copies[c].wait_recv) for c, (sx, sy) in enumerate(CORNERS)])
+    passed = {}
+    for c, (sx, sy) in enumerate(CORNERS):
+        for i, pair in enumerate(image_tiles(-sx, sy)[2:4]):
+            tile = first_in[c, :, 128 * i : 128 * i + 128].astype(F32)
+            for side, offset in enumerate(pair):
+                g = (EVENS, ODDS)[side].index(add(offset, (sx, 0)))
+                key = (sy, g, side)
+                passed[key] = tile if key not in passed else passed[key] + tile
+
+    def with_passed(tile, sy, g):
+        halves = [passed.get((sy, g, side)) for side in range(2)]
+        if halves == [None, None]:
+            return tile
+        halves = [nothing[0:64] if half is None else half for half in halves]
+        return tile + jnp.where(even[0:64], *halves)
+
     wide = imw[...]
     face_copies = [
         remote(face_out.at[FACES.index((-dx, -dy))], face_in.at[k], (face_s, face_r), k, (-dx, -dy))
         for k, (dx, dy) in enumerate(FACES)
     ]
     for first in (2, 0):
-        rows = dot(ptg[64 * first : 64 * first + 128, :], wide).astype(BF16)
-        face_out[first] = rows[0:64]
-        face_out[first + 1] = rows[64:128]
+        rows = dot(ptg[64 * first : 64 * first + 128, :], wide)
+        for k in (first, first + 1):
+            for g in range(len(PAIRS)):
+                tile = rows[64 * (k - first) : 64 * (k - first) + 64, 128 * g : 128 * g + 128]
+                if first == 2:
+                    tile = with_passed(tile, FACES[k][1], g)
+                face_out[k, :, 128 * g : 128 * g + 128] = tile.astype(BF16)
         each([((-FACES[k][0], -FACES[k][1]), face_copies[k].start) for k in (first, first + 1)])
 
     offsets = [(dx, dy) for dx in range(-3, 4) for dy in range(-3, 4) if abs(dx) + abs(dy) <= 3]
@@ -324,7 +348,6 @@
     late = []
     for c, (sx, sy) in enumerate(CORNERS):
         names = image_tiles(-sx, -sy)
-        early.extend(tiles_of(first_in.at[c], names[2:4], (sx, sy)))
         late.extend(tiles_of(rest_in.at[c], (names[0], names[1], names[4]), (sx, sy)))
 
     def gathered(total, offset, sources):
@@ -334,14 +357,17 @@
                 total = tile if total is None else total + tile
         return jnp.zeros((64, 128), F32) if total is None else total
 
-    each(
-        [((sx, sy), first_copies[c].wait_recv) for c, (sx, sy) in enumerate(CORNERS)]
-        + [(FACES[k], face_copies[k].wait_recv) for k in (0, 1)]
-    )
+    each([(FACES[k], face_copies[k].wait_recv) for k in (0, 1)])
     for offset in offsets:
         g = mine.get(offset)
         acc[at[offset]] = gathered(None if g is None else own[:, 128 * g : 128 * g + 128], offset, early)
-    each([((sx, sy), rest_copies[c].wait_recv) for c, (sx, sy) in enumerate(CORNERS)])
+    each(
+        [((-dx, -dy), facts_copies[dx, dy].wait_send) for dx, dy in DIRECTIONS]
+        + [((-sx, 0), copies_x[c].wait_send) for c, (sx, sy) in enumerate(CORNERS)]
+        + [((0, -sy), copies_y[c].wait_send) for c, (sx, sy) in enumerate(CORNERS)]
+        + [((-sx, 0), first_copies[c].wait_send) for c, (sx, sy) in enumerate(CORNERS)]
+        + [((sx, sy), rest_copies[c].wait_recv) for c, (sx, sy) in enumerate(CORNERS)]
+    )
 
     def finish(evens_first):
         def on_left(value, offset):
@@ -362,7 +388,11 @@
                 acc[at[offset]] = value
             else:
                 put(offset, value)
-        each([(FACES[k], face_copies[k].wait_recv) for k in (2, 3)])
+        each(
+            [((-sx, -sy), rest_copies[c].wait_send) for c, (sx, sy) in enumerate(CORNERS)]
+            + [((-FACES[k][0], -FACES[k][1]), face_copies[k].wait_send) for k in (0, 1)]
+            + [(FACES[k], face_copies[k].wait_recv) for k in (2, 3)]
+        )
         for offset in offsets:
             if offset in last:
                 value = acc[at[offset]]
@@ -373,14 +403,7 @@
     pl.when(par == 0)(lambda: finish(True))
     pl.when(par == 1)(lambda: finish(False))
 
-    each(
-        [((-dx, -dy), facts_copies[dx, dy].wait_send) for dx, dy in DIRECTIONS]
-        + [((-dx, -dy), face_copies[k].wait_send) for k, (dx, dy) in enumerate(FACES)]
-        + [((-sx, 0), copies_x[c].wait_send) for c, (sx, sy) in enumerate(CORNERS)]
-        + [((0, -sy), copies_y[c].wait_send) for c, (sx, sy) in enumerate(CORNERS)]
-        + [((-sx, -sy), first_copies[c].wait_send) for c, (sx, sy) in enumerate(CORNERS)]
-        + [((-sx, -sy), rest_copies[c].wait_send) for c, (sx, sy) in enumerate(CORNERS)]
-    )
+    each([((-FACES[k][0], -FACES[k][1]), face_copies[k].wait_send) for k in (2, 3)])
 
 
 def per_device(fine_matrix, prolongator, aggregate, face_links):

time: 20.2 us -> 19.6 us (0.970)
  Pallas kernels: 19.2 us -> 18.6 us
    pallas_call x1, Pallas kernels: 19.2 us -> 18.6 us  [per_device(): pl.pallas_call(functools.partial(kernel, nx, ny), out_shape=jax.ShapeDtyp...]
where the time goes in v5:
time: 19.6 us; the launch traced here: 19.5 us
  Pallas kernels  18.6 us (95%)
  local copies, waits for them, and re-layouts  0.89 us (5%)
    pallas_call x1, Pallas kernels, per_device(): pl.pallas_call(functools.partial(kernel, nx, ny), out_shape=jax.ShapeDtyp...  18.6 us
    unnamed x1, local copies, waits for them, and re-layouts  0.89 us

profile of v5, /device:TPU:39, one launch (start us, length us, event | category | flops | bytes accessed | tf_op | source)
XLA Modules:
  0.0 19.5 jit_solution(11661960077338767806)
XLA Ops:
  0.0 18.6 %galerkin.1 = bf16[1,1,7,7,64,64]{5,4,3,2,1,0:T(8,128)(2,1)S(1)} custom-call(bf16[2,2,2,7,64,64]{5,4,3,2,1,0:T(8,128)(2,1)} %a_hbm.1, bf16[2,2,2,7,64,64]{5,4,3,2,1,0:T(8,128)(2,1)} %p_hbm.1, s32[2,2,2]{2,1,0:T(2,128)} %agg_hbm.1, s32[2,2,2,6]{3,2,1,0:T(2,128)} %links_hbm.1), custom_call_target="tpu_custom_call" | custom-call | tf_op jit(solution)/shard_map/galerkin/pallas_call | solution.py:412
  18.6 0.9 %copy.6 = bf16[1,1,7,7,64,64]{5,4,3,2,1,0:T(8,128)(2,1)} copy(bf16[1,1,7,7,64,64]{5,4,3,2,1,0:T(8,128)(2,1)S(1)} %galerkin.1) | data formatting | bytes 802816

commit v6 on v5

--- a/solution.py
+++ b/solution.py
@@ -97,7 +97,7 @@
         x, y = (sx + 1) // 2, (sy + 1) // 2
         p_loads.append(pltpu.make_async_copy(p_hbm.at[x, y], p_v.at[x, y], p_sem.at[c]))
         a_loads.append(pltpu.make_async_copy(a_hbm.at[x, y], a_v.at[x, y], a_sem.at[c]))
-    for copy in (*scalar_loads, *p_loads, *a_loads):
+    for copy in (*scalar_loads, *p_loads):
         copy.start()
 
     even_row = (lax.broadcasted_iota(jnp.int32, (1, 128), 1) >= 64).astype(jnp.int32) == par
@@ -151,6 +151,8 @@
     pl.when(par == 0)(lambda: pack(True))
     pl.when(par == 1)(lambda: pack(False))
 
+    for copy in a_loads:
+        copy.start()
     pl.semaphore_wait(barrier, sum(there.astype(jnp.int32) for there in inside.values()))
 
     facts_copies = {}
@@ -397,7 +399,7 @@
             if offset in last:
                 value = acc[at[offset]]
                 for k, g in last[offset]:
-                    value += on_left(face_in[k, :, 128 * g : 128 * g + 128].astype(F32), offset)
+                    value += on_left(face_in[k, :, 128 * g : 128 * g + 128], offset).astype(F32)
                 put(offset, value)
 
     pl.when(par == 0)(lambda: finish(True))

time: 19.6 us -> 19.6 us (level)
  no operation moved by 1% of the time
where the time goes in v6:
time: 19.6 us; the launch traced here: 19.5 us
  Pallas kernels  18.6 us (95%)
  local copies, waits for them, and re-layouts  0.89 us (5%)
    pallas_call x1, Pallas kernels, per_device(): pl.pallas_call(functools.partial(kernel, nx, ny), out_shape=jax.ShapeDtyp...  18.6 us
    unnamed x1, local copies, waits for them, and re-layouts  0.89 us

profile of v6, /device:TPU:39, one launch (start us, length us, event | category | flops | bytes accessed | tf_op | source)
XLA Modules:
  0.0 19.5 jit_solution(2997418667165343181)
XLA Ops:
  0.0 18.6 %galerkin.1 = bf16[1,1,7,7,64,64]{5,4,3,2,1,0:T(8,128)(2,1)S(1)} custom-call(bf16[2,2,2,7,64,64]{5,4,3,2,1,0:T(8,128)(2,1)} %a_hbm.1, bf16[2,2,2,7,64,64]{5,4,3,2,1,0:T(8,128)(2,1)} %p_hbm.1, s32[2,2,2]{2,1,0:T(2,128)} %agg_hbm.1, s32[2,2,2,6]{3,2,1,0:T(2,128)} %links_hbm.1), custom_call_target="tpu_custom_call" | custom-call | tf_op jit(solution)/shard_map/galerkin/pallas_call | solution.py:414
  18.6 0.9 %copy.6 = bf16[1,1,7,7,64,64]{5,4,3,2,1,0:T(8,128)(2,1)} copy(bf16[1,1,7,7,64,64]{5,4,3,2,1,0:T(8,128)(2,1)S(1)} %galerkin.1) | data formatting | bytes 802816

commit v7 on v6

--- a/solution.py
+++ b/solution.py
@@ -95,7 +95,9 @@
     p_loads, a_loads = [], []
     for c, (sx, sy) in enumerate(CORNERS):
         x, y = (sx + 1) // 2, (sy + 1) // 2
-        p_loads.append(pltpu.make_async_copy(p_hbm.at[x, y], p_v.at[x, y], p_sem.at[c]))
+        for k, (z, first, count) in enumerate(((0, 0, 5), (0, 6, 1), (1, 0, 6))):
+            blocks = (x, y, z, pl.ds(first, count))
+            p_loads.append(pltpu.make_async_copy(p_hbm.at[blocks], p_v.at[blocks], p_sem.at[3 * c + k]))
         a_loads.append(pltpu.make_async_copy(a_hbm.at[x, y], a_v.at[x, y], a_sem.at[c]))
     for copy in (*scalar_loads, *p_loads):
         copy.start()
@@ -142,7 +144,8 @@
         for c, (sx, sy) in enumerate(CORNERS):
             x, y = (sx + 1) // 2, (sy + 1) // 2
             ix, iy, ox, oy = slots(sx, sy)
-            p_loads[c].wait()
+            for copy in p_loads[3 * c : 3 * c + 3]:
+                copy.wait()
             for z in range(2):
                 for j, (m, n) in enumerate(((0, 6 if z == 0 else 5), (ix, iy), (ox, oy))):
                     pair = [p_v[x, y, z, m], p_v[x, y, z, n]]
@@ -164,8 +167,9 @@
         copies_y.append(remote(raw.at[corner(sx, -sy)], raw_y.at[c], (raw_s, raw_r), 4 + c, (0, -sy)))
     each(
         [((-dx, -dy), facts_copies[dx, dy].start) for dx, dy in CORNERS + FACES]
-        + [((0, -sy), copies_y[c].start) for c, (sx, sy) in enumerate(CORNERS)]
+        + [((0, -CORNERS[c][1]), copies_y[c].start) for c in (0, 1)]
         + [((-sx, 0), copies_x[c].start) for c, (sx, sy) in enumerate(CORNERS)]
+        + [((0, -CORNERS[c][1]), copies_y[c].start) for c in (2, 3)]
     )
 
     for c, (sx, sy) in enumerate(CORNERS):
@@ -434,7 +438,7 @@
             *[pltpu.VMEM((4, 64, 384), BF16)] * 2,
             pltpu.VMEM((25, 64, 128), F32),
             dma((2,)),
-            dma((4,)),
+            dma((12,)),
             dma((4,)),
             *[dma((8,))] * 4,
             *[dma((4,))] * 6,

time: 19.6 us -> 19.7 us (level)
  no operation moved by 1% of the time
where the time goes in v7:
time: 19.7 us; the launch traced here: 19.5 us
  Pallas kernels  18.6 us (94%)
  local copies, waits for them, and re-layouts  0.89 us (5%)
    pallas_call x1, Pallas kernels, per_device(): pl.pallas_call(functools.partial(kernel, nx, ny), out_shape=jax.ShapeDtyp...  18.6 us
    unnamed x1, local copies, waits for them, and re-layouts  0.89 us

profile of v7, /device:TPU:39, one launch (start us, length us, event | category | flops | bytes accessed | tf_op | source)
XLA Modules:
  0.0 19.5 jit_solution(16007408041038577831)
XLA Ops:
  0.0 18.6 %galerkin.1 = bf16[1,1,7,7,64,64]{5,4,3,2,1,0:T(8,128)(2,1)S(1)} custom-call(bf16[2,2,2,7,64,64]{5,4,3,2,1,0:T(8,128)(2,1)} %a_hbm.1, bf16[2,2,2,7,64,64]{5,4,3,2,1,0:T(8,128)(2,1)} %p_hbm.1, s32[2,2,2]{2,1,0:T(2,128)} %agg_hbm.1, s32[2,2,2,6]{3,2,1,0:T(2,128)} %links_hbm.1), custom_call_target="tpu_custom_call" | custom-call | tf_op jit(solution)/shard_map/galerkin/pallas_call | solution.py:418
  18.6 0.9 %copy.6 = bf16[1,1,7,7,64,64]{5,4,3,2,1,0:T(8,128)(2,1)} copy(bf16[1,1,7,7,64,64]{5,4,3,2,1,0:T(8,128)(2,1)S(1)} %galerkin.1) | data formatting | bytes 802816
